TPU v7x, 32 devices: a whole 2x2x4 slice. The times are simulated.
32 devices in a mesh: grp: 2 (over y), res: 4 (over z), br: 2 (over core), aux: 2 (over x).
Axes of the slice: x: 2, y: 2, z: 4, core: 2. Of those that a mesh axis runs over, the one named last changes fastest.
Arguments:
- homolog_features: bfloat16 [32, 128, 256], P(('grp', 'br', 'aux'), 'res'), parts along dimension 0, may hold values from -6 to 6
- couple_features: bfloat16 [256, 128, 128], P(('grp', 'res'), ('br', 'aux')), parts along dimension 0, may hold values from -6 to 6
- symbol_ids: int32 [32, 128], P(('grp', 'br', 'aux'), 'res'), parts along dimension 0, may hold values from 0 to 22
- entry_present: int32 [32, 128], P(('grp', 'br', 'aux'), 'res'), parts along dimension 0, may hold values 0 or 1
- amino_present: int32 [256], P('grp'), parts along dimension 0, may hold values 0 or 1
- symbol_lookup_matrix: bfloat16 [23, 256], replicated, may hold values from -3 to 3
- horizontal_entry_matrix: bfloat16 [256, 1024], replicated, may hold values from -0.375 to 0.375
- couple_logit_matrix: bfloat16 [128, 8], replicated, may hold values from -40 to 40, as said below
- horizontal_exit_matrix: bfloat16 [256, 256], replicated, may hold values from -0.375 to 0.375
- vertical_entry_matrix: bfloat16 [256, 1024], replicated, may hold values from -0.375 to 0.375
- vertical_exit_matrix: bfloat16 [256, 256], replicated, may hold values from -0.375 to 0.375
- feedforward_first_matrix: bfloat16 [256, 1024], replicated, may hold values from -0.375 to 0.375
- feedforward_second_matrix: bfloat16 [1024, 256], replicated, may hold values from -0.1875 to 0.1875
- trimul_entry_matrix: bfloat16 [128, 640], replicated, may hold values from -0.5 to 0.5
- trimul_exit_matrix: bfloat16 [128, 128], replicated, may hold values from -0.5 to 0.5
Outputs:
- alignment_output: bfloat16 [32, 128, 256], P(('grp', 'br', 'aux'), 'res'), parts along dimension 0
- pair_output: bfloat16 [256, 128, 128], P(('grp', 'res'), ('br', 'aux')), parts along dimension 0
There are 2 independent parts, one for each index of `grp`. A program takes and returns all parts, laid end to end along the dimension named above; an argument that names none is the same for every part. Nothing has to cross between parts.
Inputs may be any that keep to these rules, and one draw needn't show every extreme that they name: `couple_logit_matrix`: a projection of the 128 pair channels onto the 8 heads.
All inputs are finite; a program needn't handle non-finite values. No bound on the sum of `entry_present` on one device may be relied on, other than what follows from the above.
Results may differ from a plain program's by a relative error of at most 0.008.
Values may be sent and summed in bfloat16 or wider, within the bound.
A program may use at most 64 MiB of HBM per device.

v0:
```python
import jax
import jax.numpy as jnp
from jax import lax
from jax.sharding import PartitionSpec as P

epsilon = 1e-05
masked_fill_value = 1000000000.0


def normalize(inputs):
    values = inputs.astype(jnp.float32)
    average = jnp.mean(values, axis=-1, keepdims=True)
    centred = values - average
    variance = jnp.mean(centred * centred, axis=-1, keepdims=True)
    return centred * lax.rsqrt(variance + epsilon)


def apply_projection(row_block, weight):
    flattened = row_block.reshape(-1, row_block.shape[-1])
    result = jnp.dot(flattened, weight, preferred_element_type=jnp.float32)
    return result.reshape(row_block.shape[:-1] + (weight.shape[1],))


def merge_block(partial_state, scores, value_rows, value_form):
    running_max, running_sum, weighted = partial_state
    new_max = jnp.maximum(running_max, jnp.max(scores, axis=-1))
    powers = jnp.exp(scores - new_max[..., None])
    running_sum = jnp.sum(powers, axis=-1)
    update = jnp.einsum(
        value_form, powers.astype(jnp.bfloat16), value_rows, preferred_element_type=jnp.float32
    )
    weighted = update
    return (new_max, running_sum, weighted)


def finish_block(partial_state, axes_order):
    running_max, running_sum, weighted = partial_state
    return weighted / jnp.transpose(running_sum, axes_order)[..., None]


def on_device(
    homolog_features,
    couple_features,
    symbol_ids,
    entry_present,
    amino_present,
    symbol_lookup_matrix,
    horizontal_entry_matrix,
    couple_logit_matrix,
    horizontal_exit_matrix,
    vertical_entry_matrix,
    vertical_exit_matrix,
    feedforward_first_matrix,
    feedforward_second_matrix,
    trimul_entry_matrix,
    trimul_exit_matrix,
):
    homolog_lines, amino_positions, feature_extent = homolog_features.shape
    heads_number = couple_logit_matrix.shape[1]
    head_width = feature_extent // heads_number
    head_scale = head_width ** (-0.5)
    pair_width = couple_features.shape[2]
    token_class_count = symbol_lookup_matrix.shape[0]
    indicator_symbols = (
        symbol_ids[..., None] == jnp.arange(token_class_count, dtype=jnp.int32)[None, None, :]
    ).astype(jnp.bfloat16)
    symbol_vectors = homolog_features.astype(jnp.float32) + jnp.einsum(
        "zas,sv->zav", indicator_symbols, symbol_lookup_matrix, preferred_element_type=jnp.float32
    )
    valid_bfloat = entry_present.astype(jnp.bfloat16)
    normed_first = normalize(symbol_vectors).astype(jnp.bfloat16)
    horizontal_combined = apply_projection(normed_first, horizontal_entry_matrix)
    horizontal_queries = (
        horizontal_combined[..., :feature_extent]
        .astype(jnp.bfloat16)
        .reshape(homolog_lines, amino_positions, heads_number, head_width)
    )
    horizontal_sigmoid = jax.nn.sigmoid(horizontal_combined[..., 3 * feature_extent :])
    pair_norm = normalize(couple_features).astype(jnp.bfloat16)
    bias_tile = jnp.einsum(
        "ijc,ch->hij", pair_norm, couple_logit_matrix, preferred_element_type=jnp.float32
    )
    pair_bias = lax.all_gather(bias_tile, ("br", "aux"), axis=2, tiled=True)
    row_init = (
        jnp.full((homolog_lines, heads_number, amino_positions), -1e30, jnp.float32),
        jnp.zeros((homolog_lines, heads_number, amino_positions), jnp.float32),
        jnp.zeros((homolog_lines, amino_positions, heads_number, head_width), jnp.float32),
    )
    partial_rows = lax.all_gather(normed_first, "res", axis=1, tiled=True)
    valid_part = lax.all_gather(valid_bfloat, "res", axis=1, tiled=True)
    key_count = partial_rows.shape[1]
    key_value_rows = apply_projection(
        partial_rows, horizontal_entry_matrix[:, feature_extent : 3 * feature_extent]
    )
    key_rows = (
        key_value_rows[..., :feature_extent]
        .astype(jnp.bfloat16)
        .reshape(homolog_lines, key_count, heads_number, head_width)
    )
    value_rows = (
        key_value_rows[..., feature_extent:]
        .astype(jnp.bfloat16)
        .reshape(homolog_lines, key_count, heads_number, head_width)
    )
    scores = (
        jnp.einsum(
            "sihd,sjhd->shij", horizontal_queries, key_rows, preferred_element_type=jnp.float32
        )
        * head_scale
    )
    scores = (
        scores
        + pair_bias[None]
        + (masked_fill_value * (valid_part.astype(jnp.float32) - 1.0))[:, None, None, :]
    )
    row_state = merge_block(row_init, scores, value_rows, "shij,sjhd->sihd")
    horizontal_context = finish_block(row_state, (0, 2, 1))
    horizontal_result = (
        horizontal_sigmoid
        * horizontal_context.reshape(homolog_lines, amino_positions, feature_extent)
    ).astype(jnp.bfloat16)
    after_row = symbol_vectors + apply_projection(horizontal_result, horizontal_exit_matrix)
    normed_second = normalize(after_row).astype(jnp.bfloat16)
    vertical_combined = apply_projection(normed_second, vertical_entry_matrix)
    vertical_queries = (
        vertical_combined[..., :feature_extent]
        .astype(jnp.bfloat16)
        .reshape(homolog_lines, amino_positions, heads_number, head_width)
    )
    column_key_rows = vertical_combined[..., feature_extent : 2 * feature_extent].astype(
        jnp.bfloat16
    )
    column_value_rows = vertical_combined[..., 2 * feature_extent : 3 * feature_extent].astype(
        jnp.bfloat16
    )
    vertical_sigmoid = jax.nn.sigmoid(vertical_combined[..., 3 * feature_extent :])
    col_init = (
        jnp.full((amino_positions, heads_number, homolog_lines), -1e30, jnp.float32),
        jnp.zeros((amino_positions, heads_number, homolog_lines), jnp.float32),
        jnp.zeros((homolog_lines, amino_positions, heads_number, head_width), jnp.float32),
    )
    key_part = lax.all_gather(column_key_rows, ("br", "aux"), axis=0, tiled=True)
    value_part = lax.all_gather(column_value_rows, ("br", "aux"), axis=0, tiled=True)
    valid_part = lax.all_gather(valid_bfloat, ("br", "aux"), axis=0, tiled=True)
    key_count = key_part.shape[0]
    key_rows = key_part.reshape(key_count, amino_positions, heads_number, head_width)
    value_rows = value_part.reshape(key_count, amino_positions, heads_number, head_width)
    scores = (
        jnp.einsum(
            "srhd,trhd->rhst", vertical_queries, key_rows, preferred_element_type=jnp.float32
        )
        * head_scale
    )
    scores = (
        scores + (masked_fill_value * (valid_part.astype(jnp.float32) - 1.0)).T[:, None, None, :]
    )
    col_state = merge_block(col_init, scores, value_rows, "rhst,trhd->srhd")
    vertical_context = finish_block(col_state, (2, 0, 1))
    vertical_result = (
        vertical_sigmoid * vertical_context.reshape(homolog_lines, amino_positions, feature_extent)
    ).astype(jnp.bfloat16)
    after_column_update = after_row + apply_projection(vertical_result, vertical_exit_matrix)
    normed_third = normalize(after_column_update).astype(jnp.bfloat16)
    hidden_units = jax.nn.relu(apply_projection(normed_third, feedforward_first_matrix)).astype(
        jnp.bfloat16
    )
    alignment_output = (
        after_column_update + apply_projection(hidden_units, feedforward_second_matrix)
    ).astype(jnp.bfloat16)
    pair_rows_dev = couple_features.shape[0]
    pair_cols_dev = couple_features.shape[1]
    valid_res = amino_present.astype(jnp.float32)
    row_valid = lax.dynamic_slice_in_dim(
        valid_res, lax.axis_index("res") * pair_rows_dev, pair_rows_dev
    )
    col_valid = lax.dynamic_slice_in_dim(
        valid_res, lax.axis_index(("br", "aux")) * pair_cols_dev, pair_cols_dev
    )
    pair_valid = row_valid[:, None] * col_valid[None, :]
    projected = jnp.einsum(
        "ijc,cd->dij",
        pair_norm,
        trimul_entry_matrix[:, : 4 * pair_width],
        preferred_element_type=jnp.float32,
    )
    left_side = (
        jax.nn.sigmoid(projected[pair_width : 2 * pair_width]) * projected[:pair_width] * pair_valid
    ).astype(jnp.bfloat16)
    right_side = (
        jax.nn.sigmoid(projected[3 * pair_width :])
        * projected[2 * pair_width : 3 * pair_width]
        * pair_valid
    ).astype(jnp.bfloat16)
    out_gate = jax.nn.sigmoid(apply_projection(pair_norm, trimul_entry_matrix[:, 4 * pair_width :]))
    left_chan, right_chan = (
        lax.all_to_all(left_side, "res", split_axis=0, concat_axis=1, tiled=True),
        lax.all_to_all(right_side, "res", split_axis=0, concat_axis=1, tiled=True),
    )
    product = jnp.einsum(
        "cki,ckj->cij",
        lax.all_gather(left_chan, ("br", "aux"), axis=2, tiled=True),
        right_chan,
        preferred_element_type=jnp.float32,
    ).astype(jnp.bfloat16)
    swapped_back = lax.all_to_all(product, "res", split_axis=1, concat_axis=0, tiled=True)
    normed_final = normalize(swapped_back.transpose(1, 2, 0)).astype(jnp.bfloat16)
    pair_output = (
        couple_features.astype(jnp.float32)
        + out_gate * apply_projection(normed_final, trimul_exit_matrix)
    ).astype(jnp.bfloat16)
    return (alignment_output, pair_output)


def solution(mesh):
    return jax.shard_map(
        on_device,
        mesh=mesh,
        in_specs=(
            P(("grp", "br", "aux"), "res", None),
            P(("grp", "res"), ("br", "aux"), None),
            P(("grp", "br", "aux"), "res"),
            P(("grp", "br", "aux"), "res"),
            P("grp"),
            P(),
            P(),
            P(),
            P(),
            P(),
            P(),
            P(),
            P(),
            P(),
            P(),
        ),
        out_specs=(P(("grp", "br", "aux"), "res", None), P(("grp", "res"), ("br", "aux"), None)),
        check_vma=False,
    )
```

profile of v0, /device:TPU:0, one launch (start us, length us, event | category | flops | bytes accessed | tf_op | source)
XLA Modules:
  0.0 149.0 jit_solution(16225407068456731938)
XLA Ops:
  7.2 0.7 convert_element_type.101
  7.9 1.2 convert_reduce_fusion
  9.1 1.3 fusion.18
  10.6 1.5 convolution_bitcast_fusion
  12.4 1.4 copy.72
  13.9 1.7 %reshape.203 = bf16[4,2,16384]{2,1,0:T(2,128)(2,1)} reshape(bf16[128,32,32]{2,1,0:T(8,128)(2,1)S(1)} %copy.72) | data formatting | bytes 524288
  15.5 6.5 %all-to-all-start = ((bf16[4,2,16384]{2,1,0:T(2,128)(2,1)}), bf16[4,2,16384]{2,1,0:T(2,128)(2,1)S(1)}, u32[]{:S(2)}, u32[]{:S(2)}) async-start(bf16[4,2,16384]{2,1,0:T(2,128)(2,1)} %reshape.203), calls=%async_computation | async-start | bytes 524288 | tf_op jit(solution)/shard_map/all_to_all | solution.py:196
  22.0 1.4 copy.74
  23.5 1.7 %reshape.205 = bf16[4,2,16384]{2,1,0:T(2,128)(2,1)} reshape(bf16[128,32,32]{2,1,0:T(8,128)(2,1)S(1)} %copy.74) | data formatting | bytes 524288
  25.8 14.4 %all_gather.21 = bf16[4,128,256]{2,1,0:T(8,128)(2,1)S(1)} all-gather(bf16[4,32,256]{2,1,0:T(8,128)(2,1)S(1)} %multiply_convert_fusion.4), channel_id=1, replica_groups=mesh['grp'=2,'res'=4,'br'=2,'aux'=2] {'res'}, dimensions={1}, use_global_device_ids=true | all-gather | bytes 327680 | tf_op jit(solution)/shard_map/all_gather | solution.py:89
  41.2 0.5 convolution_bitcast_fusion.3
  41.9 13.0 %all_gather.22 = f32[8,32,128]{1,0,2:T(8,128)S(1)} all-gather(f32[8,32,32]{1,0,2:T(8,128)S(1)} %copy.63), channel_id=1, replica_groups=mesh['grp'=2,'res'=4,'br'=2,'aux'=2] {'br','aux'}, dimensions={2}, use_global_device_ids=true | all-gather | bytes 163840 | tf_op jit(solution)/shard_map/all_gather | solution.py:83
  55.0 0.6 convert_bitcast_fusion.1
  55.7 11.3 %all-gather = bf16[4,32,4]{1,2,0:T(4,128)(2,1)S(1)} all-gather(bf16[1,32,4]{1,2,0:T(4,128)(2,1)S(1)} %get-tuple-element.10), channel_id=1, replica_groups=mesh['grp'=2,'res'=4,'br'=2,'aux'=2] {'res'}, dimensions={0}, use_global_device_ids=true | all-gather | bytes 1280 | tf_op jit(solution)/shard_map/all_gather | solution.py:90
  67.0 0.4 fusion.92
  67.6 0.4 fusion.37
  68.0 0.3 fusion.5
  69.0 1.1 fusion.94
  70.1 10.5 %all_gather.25 = bf16[16,32,256]{2,1,0:T(8,128)(2,1)S(1)} all-gather(bf16[4,32,256]{2,1,0:T(8,128)(2,1)S(1)} %get-tuple-element.7), channel_id=1, replica_groups=mesh['grp'=2,'res'=4,'br'=2,'aux'=2] {'br','aux'}, dimensions={0}, use_global_device_ids=true | all-gather | bytes 327680 | tf_op jit(solution)/shard_map/all_gather | solution.py:142
  80.6 0.4 reshape.173
  81.2 6.1 %all-gather.1 = bf16[4,4,32]{2,1,0:T(4,128)(2,1)S(1)} all-gather(bf16[1,4,32]{2,1,0:T(4,128)(2,1)S(1)} %copy-done.13), channel_id=1, replica_groups=mesh['grp'=2,'res'=4,'br'=2,'aux'=2] {'br','aux'}, dimensions={0}, use_global_device_ids=true | all-gather | bytes 1280 | tf_op jit(solution)/shard_map/all_gather | solution.py:144
  87.4 2.4 %fusion.95 = (f32[32,8,4]{2,1,0:T(8,128)}, f32[32,8,4,16]{3,2,1,0:T(4,128)}) fusion(f32[32,16]{1,0:T(8,128)S(1)} %bitcast.117, bf16[16,32,8,32]{3,2,1,0:T(8,128)(2,1)S(1)} %reshape.173, bf16[4,32,8,32]{3,2,1,0:T(8,128)(2,1)S(1)} %reshape.172), kind=kOutput, calls=%fused_computation.139 | convolution fusion | flops 1096704 | bytes 399360 | tf_op jit(solution)/shard_map/srhd,trhd->rhst/dot_general | solution.py:149
  89.9 3.4 %all-to-all-start.1 = ((bf16[4,2,16384]{2,1,0:T(2,128)(2,1)}), bf16[4,2,16384]{2,1,0:T(2,128)(2,1)S(1)}, u32[]{:S(2)}, u32[]{:S(2)}) async-start(bf16[4,2,16384]{2,1,0:T(2,128)(2,1)} %reshape.205), calls=%async_computation.1 | async-start | bytes 524288 | tf_op jit(solution)/shard_map/all_to_all | solution.py:197
  93.5 0.5 reshape.204
  94.0 0.7 copy.73
  94.7 1.2 all_to_all.36
  96.0 11.0 %all_gather.24 = bf16[16,32,256]{2,1,0:T(8,128)(2,1)S(1)} all-gather(bf16[4,32,256]{2,1,0:T(8,128)(2,1)S(1)} %get-tuple-element.8), channel_id=1, replica_groups=mesh['grp'=2,'res'=4,'br'=2,'aux'=2] {'br','aux'}, dimensions={0}, use_global_device_ids=true | all-gather | bytes 327680 | tf_op jit(solution)/shard_map/all_gather | solution.py:143
  107.0 0.4 reshape.171
  107.4 0.9 broadcast_maximum_fusion
  108.4 0.7 fusion.39
  109.0 1.1 fusion.4
  110.4 1.2 fusion.96
  111.7 2.0 %fusion.3 = f32[32,32,128]{2,1,0:T(8,128)} fusion(bf16[32,32,128]{2,1,0:T(8,128)(2,1)S(1)} %copy-done.1, f32[32,32]{1,0:T(8,128)S(1)} %copy-done.9, f32[32,32]{1,0:T(8,128)S(1)} %broadcast_multiply_fusion.2, bf16[128,640]{1,0:T(8,128)(2,1)} %param.28), kind=kOutput, calls=%fused_computation.9 | convolution fusion | flops 34471936 | bytes 827392 | tf_op jit(solution)/shard_map/dot_general | solution.py:20
  113.8 0.5 reshape.206
  114.3 0.7 copy.75
  115.0 0.5 all_to_all.40
  115.6 1.9 %convolution_convert_fusion.1 = bf16[32,128,32]{1,2,0:T(8,128)(2,1)S(1)} fusion(bf16[32,128,128]{1,2,0:T(8,128)(2,1)} %all-gather.4.cloned.1.call-done, bf16[32,128,32]{1,2,0:T(8,128)(2,1)S(1)} %all_to_all.40), kind=kOutput, calls=%fused_computation.20 | convolution fusion | flops 33685504 | bytes 1572864 | tf_op jit(solution)/shard_map/cki,ckj->cij/dot_general | solution.py:199
  117.5 1.5 copy.76
  119.0 1.7 %reshape.207 = bf16[4,2,16384]{2,1,0:T(2,128)(2,1)} reshape(bf16[128,32,32]{2,1,0:T(8,128)(2,1)S(1)} %bitcast.106) | data formatting | bytes 524288
  120.7 4.7 %all-to-all-start.2 = ((bf16[4,2,16384]{2,1,0:T(2,128)(2,1)}), bf16[4,2,16384]{2,1,0:T(2,128)(2,1)S(1)}, u32[]{:S(2)}, u32[]{:S(2)}) async-start(bf16[4,2,16384]{2,1,0:T(2,128)(2,1)} %reshape.207), calls=%async_computation.2 | async-start | bytes 524288 | tf_op jit(solution)/shard_map/all_to_all | solution.py:205
  125.4 1.1 fusion.13
  126.5 7.7 %all-to-all-done.2 = bf16[4,2,16384]{2,1,0:T(2,128)(2,1)S(1)} async-done(((bf16[4,2,16384]{2,1,0:T(2,128)(2,1)}), bf16[4,2,16384]{2,1,0:T(2,128)(2,1)S(1)}, u32[]{:S(2)}, u32[]{:S(2)}) %all-to-all-start.2) | async-done | bytes 262176 | tf_op jit(solution)/shard_map/all_to_all | solution.py:205
  134.2 0.5 reshape.208
  134.7 1.6 %convert_bitcast_fusion = f32[4,32,32,32]{3,1,2,0:T(8,128)} fusion(bf16[32,4,32,32]{3,0,2,1:T(8,128)(2,1)S(1)} %bitcast.105), kind=kLoop, calls=%fused_computation | loop fusion | flops 131072 | bytes 786432 | tf_op jit(solution)/shard_map/convert_element_type | solution.py:11
  136.4 2.1 %copy.77 = f32[4,32,32,32]{1,0,3,2:T(4,128)S(1)} copy(f32[4,32,32,32]{3,1,2,0:T(8,128)} %convert_bitcast_fusion) | data formatting | bytes 1048576 | tf_op jit(solution)/shard_map/convert_element_type | solution.py:11
  138.5 0.9 reshape.175
  139.6 0.4 multiply_reduce_fusion
  140.0 2.2 %fusion.9 = bf16[32,32,128]{2,1,0:T(8,128)(2,1)} fusion(f32[32,32,128]{2,1,0:T(8,128)} %fusion.3, bf16[32,32,128]{2,1,0:T(8,128)(2,1)S(1)} %copy-done.1, f32[128,32,32]{0,2,1:T(8,128)S(1)} %reshape.175, f32[32,32]{1,0:T(8,128)S(1)} %add_rsqrt_fusion, f32[32,32]{1,0:T(8,128)S(1)} %broadcast_multiply_fusion.1, bf16[128,128]{1,0:T(8,128)(2,1)S(1)} %copy-done.11), kind=kOutput, calls=%fused_computation.19 | convolution fusion | flops 34471936 | bytes 1613824 | tf_op jit(solution)/shard_map/dot_general | solution.py:20
  (83 shorter events, 4.4 us)
Async XLA Ops:
  7.2 61.8 %copy-start = (bf16[256,1024]{1,0:T(8,128)(2,1)S(1)}, bf16[256,1024]{1,0:T(8,128)(2,1)}, u32[]{:S(2)}) copy-start(bf16[256,1024]{1,0:T(8,128)(2,1)} %param.24) | copy-start | bytes 1572868
  10.4 30.8 %copy-start.8 = (f32[32,32]{1,0:T(8,128)}, f32[32,32]{1,0:T(8,128)S(1)}, u32[]{:S(2)}) copy-start(f32[32,32]{1,0:T(8,128)S(1)} %add_rsqrt_fusion.1) | copy-start | bytes 12292
  13.8 11.3 %copy-start.10 = (bf16[4,32,256]{2,1,0:T(8,128)(2,1)S(1)}, bf16[4,32,256]{2,1,0:T(8,128)(2,1)}, u32[]{:S(2)}) copy-start(bf16[4,32,256]{2,1,0:T(8,128)(2,1)} %param.15) | copy-start | bytes 196612
  13.8 11.3 %copy-start.12 = (bf16[23,256]{1,0:T(8,128)(2,1)S(1)}, bf16[23,256]{1,0:T(8,128)(2,1)}, u32[]{:S(2)}) copy-start(bf16[23,256]{1,0:T(8,128)(2,1)} %param.20) | copy-start | bytes 35332
  13.9 11.3 %copy-start.15 = (s32[4,32]{1,0:T(4,128)S(1)}, s32[4,32]{1,0:T(4,128)}, u32[]{:S(2)}) copy-start(s32[4,32]{1,0:T(4,128)} %param.17) | copy-start | bytes 1540
  15.5 24.7 %copy-start.2 = (bf16[256,1024]{1,0:T(8,128)(2,1)S(1)}, bf16[256,1024]{1,0:T(8,128)(2,1)}, u32[]{:S(2)}) copy-start(bf16[256,1024]{1,0:T(8,128)(2,1)} %param.21) | copy-start | bytes 1572868
  15.5 74.3 %all-to-all-start = ((bf16[4,2,16384]{2,1,0:T(2,128)(2,1)}), bf16[4,2,16384]{2,1,0:T(2,128)(2,1)S(1)}, u32[]{:S(2)}, u32[]{:S(2)}) async-start(bf16[4,2,16384]{2,1,0:T(2,128)(2,1)} %reshape.203), calls=%async_computation | async-start | bytes 524288 | tf_op jit(solution)/shard_map/all_to_all | solution.py:196
  40.2 1.0 copy-start.1
  40.2 1.0 copy-start.18
  40.8 14.3 %copy-start.14 = (s32[4,32]{1,0:T(4,128)S(1)}, s32[4,32]{1,0:T(4,128)}, u32[]{:S(2)}) copy-start(s32[4,32]{1,0:T(4,128)} %param.18) | copy-start | bytes 1540
  67.4 1.1 copy-start.16
  68.8 1.3 copy-start.6
  68.8 12.5 %copy-start.13 = (bf16[1,4,32]{2,1,0:T(4,128)(2,1)S(1)}, bf16[1,4,32]{2,1,0:T(4,128)(2,1)}, u32[]{:S(2)}) copy-start(bf16[1,4,32]{2,1,0:T(4,128)(2,1)} %get-tuple-element.9) | copy-start | bytes 772
  89.9 23.9 %all-to-all-start.1 = ((bf16[4,2,16384]{2,1,0:T(2,128)(2,1)}), bf16[4,2,16384]{2,1,0:T(2,128)(2,1)S(1)}, u32[]{:S(2)}, u32[]{:S(2)}) async-start(bf16[4,2,16384]{2,1,0:T(2,128)(2,1)} %reshape.205), calls=%async_computation.1 | async-start | bytes 524288 | tf_op jit(solution)/shard_map/all_to_all | solution.py:197
  93.3 22.3 %all-gather.4.cloned.1.call-start = ((), (), s32[]{:S(2)}) async-start(), calls=%async_computation.3 | async-start | bytes 1310720 | tf_op jit(solution)/shard_map/all_gather | solution.py:201
  96.0 12.4 %copy-start.3 = (f32[32,8,4,16]{3,2,1,0:T(4,128)S(1)}, f32[32,8,4,16]{3,2,1,0:T(4,128)}, u32[]{:S(2)}) copy-start(f32[32,8,4,16]{3,2,1,0:T(4,128)} %get-tuple-element.22) | copy-start | bytes 196612
  109.0 1.3 copy-start.7
  109.0 1.3 copy-start.17
  110.1 1.6 %copy-start.9 = (f32[32,32]{1,0:T(8,128)S(1)}, f32[32,32]{1,0:T(8,128)}, u32[]{:S(2)}) copy-start(f32[32,32]{1,0:T(8,128)} %copy-done.8) | copy-start | bytes 12292
  115.5 9.9 %copy-start.4 = (bf16[1024,256]{1,0:T(8,128)(2,1)S(1)}, bf16[1024,256]{1,0:T(8,128)(2,1)}, u32[]{:S(2)}) copy-start(bf16[1024,256]{1,0:T(8,128)(2,1)} %param.27) | copy-start | bytes 1572868
  115.5 9.9 %copy-start.5 = (bf16[256,1024]{1,0:T(8,128)(2,1)S(1)}, bf16[256,1024]{1,0:T(8,128)(2,1)}, u32[]{:S(2)}) copy-start(bf16[256,1024]{1,0:T(8,128)(2,1)} %param.26) | copy-start | bytes 1572868
  120.7 13.6 %all-to-all-start.2 = ((bf16[4,2,16384]{2,1,0:T(2,128)(2,1)}), bf16[4,2,16384]{2,1,0:T(2,128)(2,1)S(1)}, u32[]{:S(2)}, u32[]{:S(2)}) async-start(bf16[4,2,16384]{2,1,0:T(2,128)(2,1)} %reshape.207), calls=%async_computation.2 | async-start | bytes 524288 | tf_op jit(solution)/shard_map/all_to_all | solution.py:205
  138.5 1.5 %copy-start.11 = (bf16[128,128]{1,0:T(8,128)(2,1)S(1)}, bf16[128,128]{1,0:T(8,128)(2,1)}, u32[]{:S(2)}) copy-start(bf16[128,128]{1,0:T(8,128)(2,1)} %param.29) | copy-start | bytes 98308
Sparse Core Ops, SparseCore 0:
  96.2 18.3 all-gather.3
where the time goes:
time: 150 us; the launch traced here: 149 us
  blocking collectives  66.3 us (44%)
  local copies, waits for them, and re-layouts  19.6 us (13%)
  matrix products  16.8 us (11%)
  starting transfers between devices  14.8 us (10%)
  between operations  14.6 us (10%)
  other arithmetic  9.09 us (6%)
  waiting for transfers between devices  7.77 us (5%)
    all_gather x1, blocking collectives, on_device(): partial_rows = lax.all_gather(normed_first, 'res', axis=1, tiled=True)  14.4 us
    all_gather x1, blocking collectives, on_device(): pair_bias = lax.all_gather(bias_tile, ('br', 'aux'), axis=2, tiled=True)  13 us
    all_gather x1, blocking collectives, on_device(): valid_part = lax.all_gather(valid_bfloat, 'res', axis=1, tiled=True)  11.3 us
    all_gather x1, blocking collectives, on_device(): lax.all_gather(column_value_rows, ('br', 'aux'), axis=0, tiled=True)  11 us
    all_gather x1, blocking collectives, on_device(): lax.all_gather(column_key_rows, ('br', 'aux'), axis=0, tiled=True)  10.5 us
    dot_general x8, matrix products, apply_projection(): result = jnp.dot(flattened, weight, preferred_element_type=jnp.float32)  8.38 us
    all_to_all x1, waiting for transfers between devices, on_device(): lax.all_to_all(product, 'res', split_axis=1, concat_axis=0, tiled=True)  7.73 us
    unnamed x44, local copies, waits for them, and re-layouts  6.59 us
  transfers between devices with their start and end apart: 4, of which 1 were waited for; matrix products, arithmetic and copies ran while one was open for 15% of the time, Pallas kernels for 0%

commit v1 on v0

v1 whole, which is shorter than its diff:
```python
import functools

import jax
import jax.numpy as jnp
from jax import lax
from jax.experimental import pallas as pl
from jax.experimental.pallas import tpu as pltpu
from jax.sharding import PartitionSpec as P

epsilon = 1e-05
masked_fill_value = 1000000000.0
MESH = pl.DeviceIdType.MESH
f32 = jnp.float32
bf16 = jnp.bfloat16


def normalize(inputs, axis=-1):
    values = inputs.astype(f32)
    average = jnp.mean(values, axis=axis, keepdims=True)
    centred = values - average
    variance = jnp.mean(centred * centred, axis=axis, keepdims=True)
    return centred * lax.rsqrt(variance + epsilon)


def dot(a, b, contract):
    return lax.dot_general(a, b, (contract, ((), ())), preferred_element_type=f32)


class Peers:
    def __init__(self, sizes):
        self.R, self.BR, self.AX = sizes
        self.r = lax.axis_index("res")
        self.b = lax.axis_index("br")
        self.x = lax.axis_index("aux")

    def res(self, d):
        return lax.rem(self.r + d, self.R)

    def br(self, d):
        return lax.rem(self.b + d, self.BR)

    def aux(self, d):
        return lax.rem(self.x + d, self.AX)

    def res_back(self, d):
        return lax.rem(self.r + self.R - d, self.R)

    def aux_back(self, d):
        return lax.rem(self.x + self.AX - d, self.AX)

    def group(self):
        return [(bo, a) for bo in range(self.BR) for a in range(self.AX) if (bo, a) != (0, 0)]

    def barrier(self):
        semaphore = pltpu.get_barrier_semaphore()
        for d in range(1, self.R):
            pl.semaphore_signal(semaphore, inc=1, device_id={"res": self.res(d)}, device_id_type=MESH)
        for bo, a in self.group():
            pl.semaphore_signal(
                semaphore, inc=1, device_id={"br": self.br(bo), "aux": self.aux(a)}, device_id_type=MESH
            )
        pl.semaphore_wait(semaphore, self.R - 1 + self.BR * self.AX - 1)


def remote(src, dst, send, recv, device):
    copy = pltpu.make_async_remote_copy(
        src_ref=src, dst_ref=dst, send_sem=send, recv_sem=recv, device_id=device, device_id_type=MESH
    )
    copy.start()
    return copy


def first_kernel(
    sizes, rows, valid, bias, left, right,
    rows_out, row_valid, bias_out, col_valid, left_out, right_out,
    res_send, res_recv, grp_send, grp_recv, aux_send, aux_recv, br_send, br_recv,
):
    p = Peers(sizes)
    R, BR, AX = sizes
    p.barrier()
    sent = []
    arriving = []
    lefts = {}

    def relay(d, a):
        origin = (p.b, p.aux_back(a), p.res_back(d))
        src = left.at[p.r] if (d, a) == (0, 0) else left_out.at[origin]
        for bo in range(1, BR):
            copy = remote(
                src, left_out.at[origin], br_send.at[d, a, bo], br_recv.at[d, a, bo], {"br": p.br(bo)}
            )
            sent.append(copy)
            arriving.append(copy)

    def spread(d):
        origin = (p.b, p.x, p.res_back(d))
        src = left.at[p.r] if d == 0 else left_out.at[origin]
        copies = {}
        for a in range(1, AX):
            copy = remote(
                src, left_out.at[origin], aux_send.at[d, a], aux_recv.at[d, a], {"aux": p.aux(a)}
            )
            sent.append(copy)
            copies[a] = copy
        relay(d, 0)
        return copies

    for d in range(1, R):
        to = p.res(d)
        lefts[d] = remote(
            left.at[to], left_out.at[p.b, p.x, p.r], res_send.at[0, d], res_recv.at[0, d], {"res": to}
        )
        sent.append(lefts[d])
    spreads = {0: spread(0)}
    for d in range(1, R):
        to = {"res": p.res(d)}
        for n, (src, dst) in enumerate(
            ((rows, rows_out.at[p.r]), (valid, row_valid.at[p.r]), (right.at[p.res(d)], right_out.at[p.r]))
        ):
            copy = remote(src, dst, res_send.at[n + 1, d], res_recv.at[n + 1, d], to)
            sent.append(copy)
            arriving.append(copy)
    for n, (bo, a) in enumerate(p.group()):
        to = {"br": p.br(bo), "aux": p.aux(a)}
        for m, (src, dst) in enumerate(((bias, bias_out), (valid, col_valid))):
            copy = remote(src, dst.at[p.b, p.x], grp_send.at[m, n], grp_recv.at[m, n], to)
            sent.append(copy)
            arriving.append(copy)
    rows_out[p.r] = rows[...]
    row_valid[p.r] = valid[...]
    bias_out[p.b, p.x] = bias[...]
    col_valid[p.b, p.x] = valid[...]
    left_out[p.b, p.x, p.r] = left[p.r]
    right_out[p.r] = right[p.r]
    for d in range(1, R):
        lefts[d].wait_recv()
        spreads[d] = spread(d)
    for d in range(R):
        for a in range(1, AX):
            spreads[d][a].wait_recv()
            relay(d, a)
    for copy in arriving:
        copy.wait_recv()
    for copy in sent:
        copy.wait_send()


def second_kernel(
    sizes, keys, product, keys_out, product_out, res_send, res_recv, aux_send, aux_recv, br_send, br_recv
):
    p = Peers(sizes)
    R, BR, AX = sizes
    p.barrier()
    sent = []
    arriving = []

    def relay(a):
        origin = (p.b, p.aux_back(a))
        src = keys if a == 0 else keys_out.at[origin]
        for bo in range(1, BR):
            copy = remote(src, keys_out.at[origin], br_send.at[a, bo], br_recv.at[a, bo], {"br": p.br(bo)})
            sent.append(copy)
            arriving.append(copy)

    across = {}
    for a in range(1, AX):
        across[a] = remote(
            keys, keys_out.at[p.b, p.x], aux_send.at[a], aux_recv.at[a], {"aux": p.aux(a)}
        )
        sent.append(across[a])
    relay(0)
    for d in range(1, R):
        to = p.res(d)
        copy = remote(product.at[to], product_out.at[p.r], res_send.at[d], res_recv.at[d], {"res": to})
        sent.append(copy)
        arriving.append(copy)
    keys_out[p.b, p.x] = keys[...]
    product_out[p.r] = product[p.r]
    for a in range(1, AX):
        across[a].wait_recv()
        relay(a)
    for copy in arriving:
        copy.wait_recv()
    for copy in sent:
        copy.wait_send()


def call(body, name, collective, shapes, semaphores, operands):
    vmem = pl.BlockSpec(memory_space=pltpu.VMEM)
    return pl.pallas_call(
        body,
        name=name,
        out_shape=[jax.ShapeDtypeStruct(*shape) for shape in shapes],
        in_specs=[vmem] * len(operands),
        out_specs=[vmem] * len(shapes),
        scratch_shapes=[pltpu.SemaphoreType.DMA(shape) for shape in semaphores],
        compiler_params=pltpu.CompilerParams(collective_id=collective, has_side_effects=True),
    )(*operands)


def attention_row(queries, keys, values, bias, penalty, scale):
    scores = jnp.einsum("sihd,sjhd->shij", queries, keys, preferred_element_type=f32) * scale
    scores = scores + bias[None] + penalty[:, None, None, :]
    powers = jnp.exp(scores - jnp.max(scores, axis=-1, keepdims=True))
    total = jnp.sum(powers, axis=-1)
    mixed = jnp.einsum("shij,sjhd->sihd", powers.astype(bf16), values, preferred_element_type=f32)
    return mixed / jnp.transpose(total, (0, 2, 1))[..., None]


def attention_column(queries, keys, values, penalty, scale):
    scores = jnp.einsum("srhd,trhd->rhst", queries, keys, preferred_element_type=f32) * scale
    scores = scores + penalty.T[:, None, None, :]
    powers = jnp.exp(scores - jnp.max(scores, axis=-1, keepdims=True))
    total = jnp.sum(powers, axis=-1)
    mixed = jnp.einsum("rhst,trhd->srhd", powers.astype(bf16), values, preferred_element_type=f32)
    return mixed / jnp.transpose(total, (2, 0, 1))[..., None]


def on_device(
    sizes,
    homolog_features,
    couple_features,
    symbol_ids,
    entry_present,
    amino_present,
    symbol_lookup_matrix,
    horizontal_entry_matrix,
    couple_logit_matrix,
    horizontal_exit_matrix,
    vertical_entry_matrix,
    vertical_exit_matrix,
    feedforward_first_matrix,
    feedforward_second_matrix,
    trimul_entry_matrix,
    trimul_exit_matrix,
):
    R, BR, AX = sizes
    B = BR * AX
    S, A, F = homolog_features.shape
    H = couple_logit_matrix.shape[1]
    D = F // H
    scale = D ** (-0.5)
    I, J, C = couple_features.shape
    per = C // R
    tokens = symbol_lookup_matrix.shape[0]

    pair_norm = normalize(couple_features).astype(bf16).reshape(I * J, C)
    projected = dot(trimul_entry_matrix[:, : 4 * C], pair_norm, ((0,), (1,)))
    bias_own = dot(couple_logit_matrix, pair_norm, ((0,), (1,)))
    valid_res = amino_present.astype(f32)
    row_valid = lax.dynamic_slice_in_dim(valid_res, lax.axis_index("res") * I, I)
    col_valid = lax.dynamic_slice_in_dim(valid_res, lax.axis_index(("br", "aux")) * J, J)
    pair_valid = (row_valid[:, None] * col_valid[None, :]).reshape(1, I * J)
    left_own = (jax.nn.sigmoid(projected[C : 2 * C]) * projected[:C] * pair_valid).astype(bf16)
    right_own = (jax.nn.sigmoid(projected[3 * C :]) * projected[2 * C : 3 * C] * pair_valid).astype(bf16)
    out_gate = jax.nn.sigmoid(dot(pair_norm, trimul_entry_matrix[:, 4 * C :], ((1,), (0,))))

    indicator = (symbol_ids.reshape(-1, 1) == jnp.arange(tokens, dtype=jnp.int32)[None, :]).astype(bf16)
    embedded = homolog_features.astype(f32).reshape(S * A, F) + dot(indicator, symbol_lookup_matrix, ((1,), (0,)))
    normed_first = normalize(embedded).astype(bf16)
    present = entry_present.astype(f32)

    rows_all, row_present, bias_all, col_present, left_all, right_all = call(
        functools.partial(first_kernel, sizes),
        "first_exchange",
        1,
        [
            ((R, S * A, F), bf16),
            ((R, S, A), f32),
            ((BR, AX, H, I * J), f32),
            ((BR, AX, S, A), f32),
            ((BR, AX, R, per, I * J), bf16),
            ((R, per, I * J), bf16),
        ],
        [(4, R), (4, R), (2, B), (2, B), (R, AX), (R, AX), (R, AX, BR), (R, AX, BR)],
        (normed_first, present, bias_own, left_own.reshape(R, per, I * J), right_own.reshape(R, per, I * J)),
    )

    row_query_gate = dot(
        normed_first,
        jnp.concatenate([horizontal_entry_matrix[:, :F], horizontal_entry_matrix[:, 3 * F :]], axis=1),
        ((1,), (0,)),
    )
    queries = row_query_gate[:, :F].astype(bf16).reshape(S, A, H, D)
    gate = jax.nn.sigmoid(row_query_gate[:, F:])
    rows = rows_all.reshape(R, S, A, F).transpose(1, 0, 2, 3).reshape(S * R * A, F)
    key_value = dot(rows, horizontal_entry_matrix[:, F : 3 * F], ((1,), (0,))).astype(bf16)
    keys = key_value[:, :F].reshape(S, R * A, H, D)
    values = key_value[:, F:].reshape(S, R * A, H, D)
    bias = bias_all.reshape(B, H, I, J).transpose(1, 2, 0, 3).reshape(H, I, B * J)
    penalty = masked_fill_value * (row_present.transpose(1, 0, 2).reshape(S, R * A) - 1.0)
    mixed = attention_row(queries, keys, values, bias, penalty, scale)
    row_mix = (gate * mixed.reshape(S * A, F)).astype(bf16)
    after_row = embedded + dot(row_mix, horizontal_exit_matrix, ((1,), (0,)))
    normed_second = normalize(after_row).astype(bf16)
    column = dot(normed_second, vertical_entry_matrix, ((1,), (0,)))
    col_keys = column[:, F : 3 * F].astype(bf16)

    product = jnp.einsum(
        "brcki,rckj->cbij",
        left_all.reshape(B, R, per, I, J),
        right_all.reshape(R, per, I, J),
        preferred_element_type=f32,
    ).astype(bf16)
    product = product.reshape(per, R, I * J).transpose(1, 0, 2)

    keys_all, product_all = call(
        functools.partial(second_kernel, sizes),
        "second_exchange",
        2,
        [((BR, AX, S * A, 2 * F), bf16), ((R, per, I * J), bf16)],
        [(R,), (R,), (AX,), (AX,), (AX, BR), (AX, BR)],
        (col_keys, product),
    )

    queries = column[:, :F].astype(bf16).reshape(S, A, H, D)
    gate = jax.nn.sigmoid(column[:, 3 * F :])
    keys = keys_all[..., :F].reshape(B * S, A, H, D)
    values = keys_all[..., F:].reshape(B * S, A, H, D)
    penalty = masked_fill_value * (col_present.reshape(B * S, A) - 1.0)
    mixed = attention_column(queries, keys, values, penalty, scale)
    col_mix = (gate * mixed.reshape(S * A, F)).astype(bf16)
    after_col = after_row + dot(col_mix, vertical_exit_matrix, ((1,), (0,)))
    normed_third = normalize(after_col).astype(bf16)
    hidden = jax.nn.relu(dot(normed_third, feedforward_first_matrix, ((1,), (0,)))).astype(bf16)
    alignment_output = (after_col + dot(hidden, feedforward_second_matrix, ((1,), (0,)))).astype(bf16)

    normed_final = normalize(product_all.reshape(C, I * J), axis=0).astype(bf16)
    update = out_gate * dot(normed_final, trimul_exit_matrix, ((0,), (0,)))
    pair_output = (couple_features.astype(f32) + update.reshape(I, J, C)).astype(bf16)
    return (alignment_output.reshape(S, A, F), pair_output)


def solution(mesh):
    sizes = (mesh.shape["res"], mesh.shape["br"], mesh.shape["aux"])
    return jax.shard_map(
        functools.partial(on_device, sizes),
        mesh=mesh,
        in_specs=(
            P(("grp", "br", "aux"), "res", None),
            P(("grp", "res"), ("br", "aux"), None),
            P(("grp", "br", "aux"), "res"),
            P(("grp", "br", "aux"), "res"),
            P("grp"),
        )
        + (P(),) * 10,
        out_specs=(P(("grp", "br", "aux"), "res", None), P(("grp", "res"), ("br", "aux"), None)),
        check_vma=False,
    )
```

time: 150 us -> 83.3 us (0.56)
  blocking collectives: 66.3 us -> 0 us
  Pallas kernels: 0 us -> 36.2 us
  starting transfers between devices: 14.8 us -> 0 us
  between operations: 14.6 us -> 1.25 us
  waiting for transfers between devices: 7.77 us -> 0 us
  other arithmetic: 9.09 us -> 13.2 us
  local copies, waits for them, and re-layouts: 19.6 us -> 16 us
    all_gather x6 -> x0, blocking collectives: 66.3 us -> none  [the longest x1 14.4 us: on_device(): partial_rows = lax.all_gather(normed_first, 'res', axis=1, tiled=True)]
    pallas_call x0 -> x2, Pallas kernels: none -> 36.2 us  [call(): pl.pallas_call(body, name=name, out_shape=[jax.ShapeDtypeStruct(*shape) f...]
    all_to_all x3 -> x0, starting transfers between devices: 14.6 us -> none  [the longest x1 6.48 us: on_device(): lax.all_to_all(left_side, 'res', split_axis=0, concat_axis=1, tiled=True)]
    reshape x6 -> x15, local copies, waits for them, and re-layouts: 1.55 us -> 12.2 us  [the longest x1 6.43 us: on_device(): left_all.reshape(B, R, per, I, J)]
    all_to_all x3 -> x0, waiting for transfers between devices: 7.73 us -> none  [the longest x1 7.73 us: on_device(): lax.all_to_all(product, 'res', split_axis=1, concat_axis=0, tiled=True)]
    convert_element_type x5 -> x0, local copies, waits for them, and re-layouts: 7.32 us -> none  [the longest x2 2.95 us: normalize(): values = inputs.astype(jnp.float32)]
    unnamed x44 -> x42, local copies, waits for them, and re-layouts: 6.59 us -> 0.78 us
    convert_element_type x4 -> x7, other arithmetic: 2.77 us -> 6.23 us  [the longest x1 1.29 us: on_device(): pair_norm = normalize(couple_features).astype(bf16).reshape(I * J, C)]
  transfers between devices with their start and end apart: 4 -> 0, of which waited for: 1 -> 0; matrix products, arithmetic and copies ran while one was open for 15% -> 0% of each run, Pallas kernels for 0% -> 0%
where the time goes in v1:
time: 83.3 us; the launch traced here: 82.6 us
  Pallas kernels  36.2 us (43%)
  local copies, waits for them, and re-layouts  16 us (19%)
  matrix products  16 us (19%)
  other arithmetic  13.2 us (16%)
  between operations  1.25 us (2%)
    pallas_call x2, Pallas kernels, call(): pl.pallas_call(body, name=name, out_shape=[jax.ShapeDtypeStruct(*shape) f...  36.2 us
    dot_general x11, matrix products, dot(): lax.dot_general(a, b, (contract, ((), ())), preferred_element_type=f32)  8.77 us
    reshape x1, local copies, waits for them, and re-layouts, on_device(): left_all.reshape(B, R, per, I, J)  6.43 us
    dot_general x1, matrix products, on_device(): jnp.einsum('brcki,rckj->cbij', left_all.reshape(B, R, per, I, J), right_a...  3.48 us
    reduce_sum x5, other arithmetic, normalize(): variance = jnp.mean(centred * centred, axis=axis, keepdims=True)  2.9 us
    reduce_sum x2, other arithmetic, normalize(): average = jnp.mean(values, axis=axis, keepdims=True)  2.22 us
    dot_general x1, matrix products, attention_column(): jnp.einsum('rhst,trhd->srhd', powers.astype(bf16), values, preferred_elem...  2.01 us
    reshape x2, local copies, waits for them, and re-layouts, on_device(): product = product.reshape(per, R, I * J).transpose(1, 0, 2)  1.84 us

profile of v1, /device:TPU:0, one launch (start us, length us, event | category | flops | bytes accessed | tf_op | source)
XLA Modules:
  0.0 82.6 jit_solution(12941898482095740884)
XLA Ops:
  0.7 0.8 convert_element_type.77
  1.7 1.2 %convert_reduce_fusion = f32[32,32]{1,0:T(8,128)S(1)} fusion(bf16[32,32,128]{2,1,0:T(8,128)(2,1)} %param.16), kind=kLoop, calls=%fused_computation.33 | loop fusion | flops 261120 | bytes 266240 | tf_op jit(solution)/shard_map/reduce_sum | solution.py:19
  2.9 1.3 %fusion.21 = f32[32,32]{1,0:T(8,128)S(1)} fusion(bf16[32,32,128]{2,1,0:T(8,128)(2,1)} %param.16, f32[32,32]{1,0:T(8,128)S(1)} %broadcast_multiply_fusion.1), kind=kLoop, calls=%fused_computation.36 | loop fusion | flops 523264 | bytes 270336 | tf_op jit(solution)/shard_map/reduce_sum | solution.py:21
  4.2 1.3 %fusion.22 = bf16[32,32,128]{2,1,0:T(8,128)(2,1)S(1)} fusion(bf16[32,32,128]{2,1,0:T(8,128)(2,1)} %param.16, f32[32,32]{1,0:T(8,128)S(1)} %add_rsqrt_fusion, f32[32,32]{1,0:T(8,128)S(1)} %broadcast_multiply_fusion.1), kind=kLoop, calls=%fused_computation.37 | loop fusion | flops 524288 | bytes 532480 | tf_op jit(solution)/shard_map/convert_element_type | solution.py:247
  5.5 1.4 %convolution_bitcast_fusion = f32[512,1024]{1,0:T(8,128)S(1)} fusion(bf16[1024,128]{1,0:T(8,128)(2,1)S(1)} %bitcast.81, bf16[128,640]{1,0:T(8,128)(2,1)} %param.28), kind=kOutput, calls=%fused_computation.3 | convolution fusion | flops 134217728 | bytes 2490368 | tf_op jit(solution)/shard_map/dot_general | solution.py:26
  6.9 1.1 %fusion.25 = (bf16[128,1024]{1,0:T(8,128)(2,1)}, bf16[128,1024]{1,0:T(8,128)(2,1)}) fusion(f32[512,1024]{1,0:T(8,128)S(1)} %convolution_bitcast_fusion, f32[1024]{0:T(1024)S(1)} %mul.164), kind=kLoop, calls=%fused_computation.41 | loop fusion | flops 1572864 | bytes 2625536 | tf_op jit(solution)/shard_map/convert_element_type | solution.py:255
  8.0 0.3 fusion.86
  8.4 0.2 multiply_reduce_fusion.3
  8.6 0.7 multiply_convert_fusion.2.rows
  9.3 0.8 convolution_bitcast_fusion.3.bias
  10.1 0.6 convert_element_type.74.valid
  10.7 24.6 %first_exchange.1 = (bf16[4,128,256]{2,1,0:T(8,128)(2,1)}, f32[4,4,32]{2,1,0:T(4,128)}, f32[2,2,8,1024]{3,2,1,0:T(8,128)}, f32[2,2,4,32]{3,2,1,0:T(4,128)}, bf16...) custom-call(bf16[128,256]{1,0:T(8,128)(2,1)} %multiply_convert_fusion.2.rows, ...), custom_call_target="tpu_custom_call" | custom-call | tf_op jit(solution)/shard_map/first_exchange/pallas_call | solution.py:190
  35.3 6.4 %reshape.188 = bf16[4,4,32,32,32]{4,3,2,1,0:T(8,128)(2,1)} reshape(bf16[2,2,4,32,1024]{4,3,2,1,0:T(8,128)(2,1)} %get-tuple-element.13) | data formatting | bytes 2097152 | tf_op jit(solution)/shard_map/reshape | solution.py:301
  41.7 0.8 reshape.189
  42.5 3.5 %bitcast_convert_fusion = bf16[32,4,32,32]{3,2,1,0:T(8,128)(2,1)S(1)} fusion(bf16[4,4,32,32,32]{4,3,2,1,0:T(8,128)(2,1)} %reshape.188, bf16[4,32,32,32]{3,2,1,0:T(8,128)(2,1)S(1)} %reshape.189), kind=kOutput, calls=%fused_computation.2 | convolution fusion | flops 33685504 | bytes 1572864 | tf_op jit(solution)/shard_map/brcki,rckj->cbij/dot_general | solution.py:299
  46.0 1.0 %reshape.202 = bf16[32,4,1024]{2,1,0:T(4,128)(2,1)S(1)} reshape(bf16[32,4,32,32]{3,2,1,0:T(8,128)(2,1)S(1)} %bitcast_convert_fusion) | data formatting | bytes 524288 | tf_op jit(solution)/shard_map/reshape | solution.py:305
  47.1 0.8 copy.82
  47.9 1.0 %copy.29 = bf16[4,4,32,256]{3,2,0,1:T(8,128)(2,1)S(1)} copy(bf16[4,4,32,256]{3,2,1,0:T(8,128)(2,1)} %bitcast.90) | data formatting | bytes 524288 | tf_op jit(solution)/shard_map/reshape | solution.py:286
  48.8 1.2 %convolution_convert_fusion = bf16[512,512]{1,0:T(8,128)(2,1)S(1)} fusion(bf16[512,256]{1,0:T(8,128)(2,1)S(1)} %bitcast.89, bf16[256,1024]{1,0:T(8,128)(2,1)} %param.21), kind=kOutput, calls=%fused_computation.4 | convolution fusion | flops 134479872 | bytes 1048576 | tf_op jit(solution)/shard_map/dot_general | solution.py:26
  50.5 0.3 copy.81
  50.9 0.3 add.130
  51.3 1.0 %fusion.84 = (bf16[256,256]{1,0:T(8,128)(2,1)S(1)}, bf16[256,256]{1,0:T(8,128)(2,1)S(1)}) fusion(bf16[256,1024]{1,0:T(8,128)(2,1)} %param.21), kind=kLoop, calls=%fused_computation.127 | loop fusion | bytes 524288 | tf_op jit(solution)/shard_map/slice | solution.py:281
  52.3 0.2 fusion.42
  52.5 0.7 copy-done.6
  53.4 0.4 fusion.87
  53.7 0.4 fusion.36
  54.4 0.3 fusion.9
  54.7 0.2 copy.37
  54.9 0.2 reshape.187
  55.2 0.3 fusion.88
  55.4 0.2 multiply_reduce_fusion.2
  55.6 1.1 %fusion.89 = (bf16[128,1024]{1,0:T(8,128)(2,1)S(1)}, f32[128,1024]{1,0:T(8,128)}) fusion(bf16[256,1024]{1,0:T(8,128)(2,1)S(1)} %copy-done, f32[128,256]{1,0:T(8,128)S(1)} %get-tuple-element.33, f32[128]{0:T(128)S(1)} %add_rsqrt_fusion.3, f32[128]{0:T(128)S(1)} %broadcast_multiply_fusion.4), kind=kOutput, calls=%fused_computation.132 | convolution fusion | flops 67338240 | bytes 1442816 | tf_op jit(solution)/shard_map/dot_general | solution.py:26
  56.7 0.7 slice.84.keys
  57.4 11.6 %second_exchange.1 = (bf16[2,2,128,512]{3,2,1,0:T(8,128)(2,1)}, bf16[4,32,1024]{2,1,0:T(8,128)(2,1)}) custom-call(bf16[128,512]{1,0:T(8,128)(2,1)} %slice.84.keys, bf16[4,32,1024]{2,1,0:T(8,128)(2,1)} %bitcast.88), custom_call_target="tpu_custom_call" | custom-call | tf_op jit(solution)/shard_map/second_exchange/pallas_call | solution.py:190
  69.0 1.1 %convert_reduce_fusion.1 = f32[1024]{0:T(1024)S(1)} fusion(bf16[4,32,1024]{2,1,0:T(8,128)(2,1)} %get-tuple-element.17), kind=kLoop, calls=%fused_computation.73 | loop fusion | flops 261120 | bytes 266240 | tf_op jit(solution)/shard_map/reduce_sum | solution.py:19
  70.1 1.0 %multiply_reduce_fusion = f32[1024]{0:T(1024)S(1)} fusion(bf16[4,32,1024]{2,1,0:T(8,128)(2,1)} %get-tuple-element.17, f32[1024]{0:T(1024)S(1)} %broadcast_multiply_fusion.2), kind=kLoop, calls=%fused_computation.57 | loop fusion | flops 523264 | bytes 270336 | tf_op jit(solution)/shard_map/reduce_sum | solution.py:21
  71.1 1.0 %fusion.35 = bf16[128,1024]{1,0:T(8,128)(2,1)S(1)} fusion(bf16[4,32,1024]{2,1,0:T(8,128)(2,1)} %get-tuple-element.17, f32[1024]{0:T(1024)S(1)} %add_rsqrt_fusion.1, f32[1024]{0:T(1024)S(1)} %broadcast_multiply_fusion.2), kind=kLoop, calls=%fused_computation.55 | loop fusion | flops 524288 | bytes 532480 | tf_op jit(solution)/shard_map/convert_element_type | solution.py:328
  72.1 1.1 %fusion.7 = f32[1024,128]{1,0:T(8,128)S(1)} fusion(bf16[1024,128]{1,0:T(8,128)(2,1)S(1)} %bitcast.83, bf16[128,640]{1,0:T(8,128)(2,1)} %param.28), kind=kOutput, calls=%fused_computation.11 | convolution fusion | flops 33947648 | bytes 819200 | tf_op jit(solution)/shard_map/dot_general | solution.py:26
  73.2 0.3 convolution_multiply_fusion.1
  73.5 0.8 fusion.23
  74.3 0.4 reshape.193
  75.0 1.1 %fusion.90 = (f32[32,8,4]{2,1,0:T(8,128)S(1)}, f32[32,8,4,16]{3,2,1,0:T(4,128)S(1)}) fusion(f32[32,16]{1,0:T(8,128)S(1)} %copy.43, bf16[16,32,8,32]{3,2,1,0:T(8,128)(2,1)S(1)} %reshape.193, bf16[4,32,8,32]{3,2,1,0:T(8,128)(2,1)S(1)} %reshape.192), kind=kOutput, calls=%fused_computation.133 | convolution fusion | flops 1096704 | bytes 399360 | tf_op jit(solution)/shard_map/srhd,trhd->rhst/dot_general | solution.py:211
  76.1 1.3 %fusion.38 = f32[32,8,4]{2,1,0:T(8,128)} fusion(f32[32,8,4,16]{3,2,1,0:T(4,128)S(1)} %get-tuple-element.37, f32[32,8,4]{2,1,0:T(8,128)S(1)} %get-tuple-element.36), kind=kLoop, calls=%fused_computation.62 | loop fusion | flops 31744 | bytes 73728 | tf_op jit(solution)/shard_map/reduce_sum | solution.py:214
  77.4 0.4 reshape.191
  77.9 2.0 %fusion.8 = f32[4,32,8,32]{3,0,2,1:T(4,128)S(1)} fusion(bf16[16,32,8,32]{3,2,1,0:T(8,128)(2,1)S(1)} %reshape.191, f32[32,8,4,16]{3,2,1,0:T(4,128)S(1)} %get-tuple-element.37, f32[4,32,8]{0,2,1:T(8,128)} %bitcast.91, f32[32,8,4]{2,1,0:T(8,128)} %copy-done.10), kind=kOutput, calls=%fused_computation.13 | convolution fusion | flops 1114112 | bytes 466944 | tf_op jit(solution)/shard_map/rhst,trhd->srhd/dot_general | solution.py:215
  80.0 0.2 reshape.194
  80.1 1.2 %fusion.91 = (f32[128]{0:T(128)S(1)}, f32[128,256]{1,0:T(8,128)S(1)}) fusion(f32[128,256]{1,0:T(8,128)S(1)} %get-tuple-element.33, bf16[256,256]{1,0:T(8,128)(2,1)S(1)} %copy-done.20, f32[128,256]{1,0:T(8,128)S(1)} %reshape.194, f32[128,1024]{1,0:T(8,128)} %get-tuple-element.35), kind=kOutput, calls=%fused_computation.134 | convolution fusion | flops 17006464 | bytes 655872 | tf_op jit(solution)/shard_map/dot_general | solution.py:26
  81.5 1.1 %fusion.15 = bf16[128,256]{1,0:T(8,128)(2,1)} fusion(f32[128,256]{1,0:T(8,128)S(1)} %get-tuple-element.39, bf16[1024,256]{1,0:T(8,128)(2,1)S(1)} %copy-done.3, bf16[256,1024]{1,0:T(8,128)(2,1)S(1)} %copy-done.4, f32[128]{0:T(128)S(1)} %add_rsqrt_fusion.2, f32[128]{0:T(128)S(1)} %broadcast_multiply_fusion.3), kind=kOutput, calls=%fused_computation.26 | convolution fusion | flops 134643712 | bytes 1246208 | tf_op jit(solution)/shard_map/dot_general | solution.py:26
  (73 shorter events, 1.9 us)
Async XLA Ops:
  0.6 55.0 %copy-start = (bf16[256,1024]{1,0:T(8,128)(2,1)S(1)}, bf16[256,1024]{1,0:T(8,128)(2,1)}, u32[]{:S(2)}) copy-start(bf16[256,1024]{1,0:T(8,128)(2,1)} %param.24) | copy-start | bytes 1572868
  0.6 7.3 %copy-start.17 = (s32[4,32]{1,0:T(4,128)S(1)}, s32[4,32]{1,0:T(4,128)}, u32[]{:S(2)}) copy-start(s32[4,32]{1,0:T(4,128)} %param.17) | copy-start | bytes 1540
  0.7 7.4 %copy-start.11 = (bf16[4,32,256]{2,1,0:T(8,128)(2,1)S(1)}, bf16[4,32,256]{2,1,0:T(8,128)(2,1)}, u32[]{:S(2)}) copy-start(bf16[4,32,256]{2,1,0:T(8,128)(2,1)} %param.15) | copy-start | bytes 196612
  0.7 7.4 %copy-start.13 = (bf16[23,256]{1,0:T(8,128)(2,1)S(1)}, bf16[23,256]{1,0:T(8,128)(2,1)}, u32[]{:S(2)}) copy-start(bf16[23,256]{1,0:T(8,128)(2,1)} %param.20) | copy-start | bytes 35332
  0.7 8.6 %copy-start.16 = (bf16[128,8]{0,1:T(8,128)(2,1)S(1)}, bf16[128,8]{0,1:T(8,128)(2,1)}, u32[]{:S(2)}) copy-start(bf16[128,8]{0,1:T(8,128)(2,1)} %param.22) | copy-start | bytes 6148
  0.7 9.4 %copy-start.18 = (s32[4,32]{1,0:T(4,128)S(1)}, s32[4,32]{1,0:T(4,128)}, u32[]{:S(2)}) copy-start(s32[4,32]{1,0:T(4,128)} %param.18) | copy-start | bytes 1540
  35.3 6.4 %copy-start.8 = (bf16[4,32,1024]{2,1,0:T(8,128)(2,1)S(1)}, bf16[4,32,1024]{2,1,0:T(8,128)(2,1)}, u32[]{:S(2)}) copy-start(bf16[4,32,1024]{2,1,0:T(8,128)(2,1)} %get-tuple-element.14) | copy-start | bytes 786436
  46.0 4.4 %copy-start.9 = (f32[2,2,8,1024]{3,2,1,0:T(8,128)S(1)}, f32[2,2,8,1024]{3,2,1,0:T(8,128)}, u32[]{:S(2)}) copy-start(f32[2,2,8,1024]{3,2,1,0:T(8,128)} %get-tuple-element.11) | copy-start | bytes 393220
  46.0 5.1 %copy-start.15 = (f32[4,4,32]{2,1,0:T(4,128)S(1)}, f32[4,4,32]{2,1,0:T(4,128)}, u32[]{:S(2)}) copy-start(f32[4,4,32]{2,1,0:T(4,128)} %get-tuple-element.12) | copy-start | bytes 6148
  46.0 6.3 %copy-start.2 = (bf16[128,256]{1,0:T(8,128)(2,1)S(1)}, bf16[128,256]{1,0:T(8,128)(2,1)}, u32[]{:S(2)}) copy-start(bf16[128,256]{1,0:T(8,128)(2,1)} %multiply_convert_fusion.2.rows) | copy-start | bytes 196612
  51.3 3.9 %copy-start.19 = (bf16[256,256]{1,0:T(8,128)(2,1)S(1)}, bf16[256,256]{1,0:T(8,128)(2,1)}, u32[]{:S(2)}) copy-start(bf16[256,256]{1,0:T(8,128)(2,1)} %param.23) | copy-start | bytes 393220
  52.5 0.7 copy-start.6
  53.4 1.8 %copy-start.7 = (f32[128,512]{1,0:T(8,128)S(1)}, f32[128,512]{1,0:T(8,128)}, u32[]{:S(2)}) copy-start(f32[128,512]{1,0:T(8,128)} %copy-done.6) | copy-start | bytes 786436
  54.7 18.5 %copy-start.12 = (bf16[128,128]{1,0:T(8,128)(2,1)S(1)}, bf16[128,128]{1,0:T(8,128)(2,1)}, u32[]{:S(2)}) copy-start(bf16[128,128]{1,0:T(8,128)(2,1)} %param.29) | copy-start | bytes 98308
  54.9 18.5 %copy-start.1 = (bf16[32,32,128]{2,1,0:T(8,128)(2,1)S(1)}, bf16[32,32,128]{2,1,0:T(8,128)(2,1)}, u32[]{:S(2)}) copy-start(bf16[32,32,128]{2,1,0:T(8,128)(2,1)} %param.16) | copy-start | bytes 786436
  69.0 5.3 %copy-start.5 = (bf16[2,2,128,512]{3,2,1,0:T(8,128)(2,1)S(1)}, bf16[2,2,128,512]{3,2,1,0:T(8,128)(2,1)}, u32[]{:S(2)}) copy-start(bf16[2,2,128,512]{3,2,1,0:T(8,128)(2,1)} %get-tuple-element.15) | copy-start | bytes 1572868
  70.0 4.9 %copy-start.14 = (f32[2,2,4,32]{3,2,1,0:T(4,128)S(1)}, f32[2,2,4,32]{3,2,1,0:T(4,128)}, u32[]{:S(2)}) copy-start(f32[2,2,4,32]{3,2,1,0:T(4,128)} %get-tuple-element.16) | copy-start | bytes 6148
  76.1 1.3 %copy-start.10 = (f32[32,8,4]{2,1,0:T(8,128)}, f32[32,8,4]{2,1,0:T(8,128)S(1)}, u32[]{:S(2)}) copy-start(f32[32,8,4]{2,1,0:T(8,128)S(1)} %get-tuple-element.36) | copy-start | bytes 12292
  77.8 2.3 %copy-start.20 = (bf16[256,256]{1,0:T(8,128)(2,1)S(1)}, bf16[256,256]{1,0:T(8,128)(2,1)}, u32[]{:S(2)}) copy-start(bf16[256,256]{1,0:T(8,128)(2,1)} %param.25) | copy-start | bytes 393220
  77.9 3.7 %copy-start.3 = (bf16[1024,256]{1,0:T(8,128)(2,1)S(1)}, bf16[1024,256]{1,0:T(8,128)(2,1)}, u32[]{:S(2)}) copy-start(bf16[1024,256]{1,0:T(8,128)(2,1)} %param.27) | copy-start | bytes 1572868
  77.9 3.7 %copy-start.4 = (bf16[256,1024]{1,0:T(8,128)(2,1)S(1)}, bf16[256,1024]{1,0:T(8,128)(2,1)}, u32[]{:S(2)}) copy-start(bf16[256,1024]{1,0:T(8,128)(2,1)} %param.26) | copy-start | bytes 1572868

commit v2 on v1

v2 whole, which is shorter than its diff:
```python
import functools

import jax
import jax.numpy as jnp
from jax import lax
from jax.experimental import pallas as pl
from jax.experimental.pallas import tpu as pltpu
from jax.sharding import PartitionSpec as P

epsilon = 1e-05
masked_fill_value = 1000000000.0
MESH = pl.DeviceIdType.MESH
f32 = jnp.float32
bf16 = jnp.bfloat16


def normalize(inputs, axis=-1):
    values = inputs.astype(f32)
    average = jnp.mean(values, axis=axis, keepdims=True)
    centred = values - average
    variance = jnp.mean(centred * centred, axis=axis, keepdims=True)
    return centred * lax.rsqrt(variance + epsilon)


def dot(a, b, contract):
    return lax.dot_general(a, b, (contract, ((), ())), preferred_element_type=f32)


class Peers:
    def __init__(self, sizes):
        self.R, self.BR, self.AX = sizes
        self.r = lax.axis_index("res")
        self.b = lax.axis_index("br")
        self.x = lax.axis_index("aux")

    def res(self, d):
        return lax.rem(self.r + d, self.R)

    def br(self, d):
        return lax.rem(self.b + d, self.BR)

    def aux(self, d):
        return lax.rem(self.x + d, self.AX)

    def res_back(self, d):
        return lax.rem(self.r + self.R - d, self.R)

    def aux_back(self, d):
        return lax.rem(self.x + self.AX - d, self.AX)

    def group(self):
        return [(bo, a) for bo in range(self.BR) for a in range(self.AX) if (bo, a) != (0, 0)]

    def greet(self):
        semaphore = pltpu.get_barrier_semaphore()
        for d in range(1, self.R):
            pl.semaphore_signal(semaphore, inc=1, device_id={"res": self.res(d)}, device_id_type=MESH)
        for bo, a in self.group():
            pl.semaphore_signal(
                semaphore, inc=1, device_id={"br": self.br(bo), "aux": self.aux(a)}, device_id_type=MESH
            )

    def met(self):
        pl.semaphore_wait(pltpu.get_barrier_semaphore(), self.R - 1 + self.BR * self.AX - 1)


def remote(src, dst, send, recv, device):
    copy = pltpu.make_async_remote_copy(
        src_ref=src, dst_ref=dst, send_sem=send, recv_sem=recv, device_id=device, device_id_type=MESH
    )
    copy.start()
    return copy


def iota(shape, axis):
    return lax.broadcasted_iota(jnp.int32, shape, axis)


def by_head(rows, heads):
    n, width = rows.shape
    mask = (iota((heads, width), 1) // (width // heads) == iota((heads, width), 0)).astype(f32)
    return (rows[:, None, :] * mask[None]).reshape(n * heads, width)


def from_head(rows, heads):
    n, width = rows.shape
    mask = (iota((heads, width), 1) // (width // heads) == iota((heads, width), 0)).astype(f32)
    return jnp.sum(rows.reshape(n // heads, heads, width) * mask[None], axis=1)


def attend(scores, values, heads):
    powers = jnp.exp(scores - jnp.max(scores, axis=-1, keepdims=True))
    total = jnp.sum(powers, axis=-1, keepdims=True)
    mixed = dot(powers.astype(bf16), values, ((1,), (0,)))
    return from_head(mixed / total, heads)


def joined(pieces, lanes):
    per_tile = 128 // lanes
    tiles = []
    for first in range(0, len(pieces), per_tile):
        tile = pieces[first]
        group = iota(tile.shape, 1) // lanes
        for k in range(1, min(per_tile, len(pieces) - first)):
            tile = jnp.where(group == k, pieces[first + k], tile)
        tiles.append(tile)
    return tiles[0] if len(tiles) == 1 else jnp.concatenate(tiles, axis=1)


def block_kernel(
    sizes, dims,
    homolog, couple, indicator, present, pair_valid, table, row_in, pair_in, row_exit, col_in, col_exit,
    feed_first, feed_second, gate_in, tri_exit,
    alignment, pair,
    rows_own, bias_own, left_own, right_own, keys_own, product_own,
    rows_all, row_present, bias_all, col_present, left_all, right_all, keys_all, product_all,
    embedded_s, pair_norm_s, gate_s, bias_s, key_value_s, left_s, right_s, product_s, update_s, context_s,
    res_send, res_recv, grp_send, grp_recv, aux_send, aux_recv, br_send, br_recv,
    across_send, across_recv, over_send, over_recv,
):
    p = Peers(sizes)
    R, BR, AX = sizes
    B = BR * AX
    S, A, F, H, I, J, C, per, T, N = dims
    scale = (F // H) ** (-0.5)
    Q = 128 // J
    M = J // Q
    p.greet()
    sent = []
    arriving = {"rows": [], "bias": [], "right": [], "left": [], "keys": [], "product": []}

    pair_norm = normalize(couple[...]).astype(bf16)
    pair_norm_s[...] = pair_norm
    for side, own in ((0, left_own), (1, right_own)):
        first = 2 * side * C
        value = dot(pair_in[first : first + C, :], pair_norm, ((1,), (1,)))
        sigma = jax.nn.sigmoid(dot(pair_in[first + C : first + 2 * C, :], pair_norm, ((1,), (1,))))
        value = sigma * value * pair_valid[...]
        for n in range(R):
            for t in range(T):
                own[n, t] = value[n * per : (n + 1) * per, t * 128 : (t + 1) * 128].astype(bf16)
    bias_own[...] = dot(pair_in[4 * C :, :], pair_norm, ((1,), (1,)))
    embedded = homolog[...].astype(f32) + dot(indicator[...], table[...], ((1,), (0,)))
    embedded_s[...] = embedded
    normed_first = normalize(embedded).astype(bf16)
    rows_own[...] = normed_first

    p.met()

    def relay(d, a):
        origin = (p.b, p.aux_back(a), p.res_back(d))
        src = left_own.at[p.r] if (d, a) == (0, 0) else left_all.at[origin]
        for bo in range(1, BR):
            copy = remote(
                src, left_all.at[origin], br_send.at[d, a, bo], br_recv.at[d, a, bo], {"br": p.br(bo)}
            )
            sent.append(copy)
            arriving["left"].append(copy)

    def spread(d):
        origin = (p.b, p.x, p.res_back(d))
        src = left_own.at[p.r] if d == 0 else left_all.at[origin]
        copies = {}
        for a in range(1, AX):
            copies[a] = remote(
                src, left_all.at[origin], aux_send.at[d, a], aux_recv.at[d, a], {"aux": p.aux(a)}
            )
            sent.append(copies[a])
        relay(d, 0)
        return copies

    def to_res(index, kind, pairs):
        for d in range(1, R):
            for n, (src, dst) in enumerate(pairs(p.res(d))):
                copy = remote(
                    src, dst, res_send.at[index + n, d], res_recv.at[index + n, d], {"res": p.res(d)}
                )
                sent.append(copy)
                arriving[kind].append(copy)

    lefts = {}
    for d in range(1, R):
        lefts[d] = remote(
            left_own.at[p.res(d)], left_all.at[p.b, p.x, p.r], res_send.at[0, d], res_recv.at[0, d],
            {"res": p.res(d)},
        )
        sent.append(lefts[d])
    spreads = {0: spread(0)}
    to_res(1, "rows", lambda to: ((rows_own, rows_all.at[p.r]), (present.at[0], row_present.at[p.r])))
    for n, (bo, a) in enumerate(p.group()):
        to = {"br": p.br(bo), "aux": p.aux(a)}
        for m, (src, dst) in enumerate(((bias_own, bias_all), (present.at[1], col_present))):
            copy = remote(src, dst.at[p.b, p.x], grp_send.at[m, n], grp_recv.at[m, n], to)
            sent.append(copy)
            arriving["bias"].append(copy)
    to_res(3, "right", lambda to: ((right_own.at[to], right_all.at[p.r]),))
    rows_all[p.r] = rows_own[...]
    row_present[p.r] = present[0]
    bias_all[p.b, p.x] = bias_own[...]
    col_present[p.b, p.x] = present[1]
    left_all[p.b, p.x, p.r] = left_own[p.r]
    right_all[p.r] = right_own[p.r]

    query = dot(normed_first, row_in[:, :F], ((1,), (0,))).astype(bf16).astype(f32)
    row_gate = jax.nn.sigmoid(dot(normed_first, row_in[:, 3 * F :], ((1,), (0,))))
    gate_s[...] = jax.nn.sigmoid(dot(pair_norm, gate_in[...], ((1,), (0,))))

    for d in range(1, R):
        lefts[d].wait_recv()
        spreads[d] = spread(d)
    for copy in arriving["bias"]:
        copy.wait_recv()
    for t in range(T):
        for q in range(Q):
            pieces = []
            for b in range(B):
                tile = bias_all[b // AX, b % AX, :, t * 128 : (t + 1) * 128]
                turn = (b - q) % Q * J
                pieces.append(pltpu.roll(tile, turn, 1) if turn else tile)
            row = (t * Q + q) * H
            bias_s[row : row + H, :] = joined(pieces, J)
    for d in range(R):
        for a in range(1, AX):
            spreads[d][a].wait_recv()
            relay(d, a)

    for copy in arriving["rows"]:
        copy.wait_recv()
    key_value_s[...] = (
        dot(rows_all[...].reshape(R * S * A, F), row_in[:, F : 3 * F], ((1,), (0,)))
        .astype(bf16)
        .reshape(R, S * A, 2 * F)
    )
    presence = joined([row_present[n] for n in range(R)], A)
    for s in range(S):
        mine = slice(s * A, (s + 1) * A)
        keys = key_value_s[:, mine, :F].reshape(R * A, F)
        values = key_value_s[:, mine, F:].reshape(R * A, F)
        scores = dot(by_head(query[mine], H).astype(bf16), keys, ((1,), (1,))) * scale
        scores = scores + bias_s[...] + masked_fill_value * (presence[s : s + 1] - 1.0)
        context_s[mine, :] = attend(scores, values, H)
    row_mix = (row_gate * context_s[...]).astype(bf16)
    after_row = embedded_s[...] + dot(row_mix, row_exit[...], ((1,), (0,)))
    normed_second = normalize(after_row).astype(bf16)
    keys_own[...] = dot(normed_second, col_in[:, F : 3 * F], ((1,), (0,))).astype(bf16).reshape(S, A, 2 * F)
    query = dot(normed_second, col_in[:, :F], ((1,), (0,))).astype(bf16).astype(f32)
    col_gate = jax.nn.sigmoid(dot(normed_second, col_in[:, 3 * F :], ((1,), (0,))))

    def pass_on(a):
        origin = (p.b, p.aux_back(a))
        src = keys_own if a == 0 else keys_all.at[origin]
        for bo in range(1, BR):
            copy = remote(src, keys_all.at[origin], over_send.at[a, bo], over_recv.at[a, bo], {"br": p.br(bo)})
            sent.append(copy)
            arriving["keys"].append(copy)

    across = {}
    for a in range(1, AX):
        across[a] = remote(
            keys_own, keys_all.at[p.b, p.x], across_send.at[a], across_recv.at[a], {"aux": p.aux(a)}
        )
        sent.append(across[a])
    pass_on(0)
    keys_all[p.b, p.x] = keys_own[...]

    for copy in arriving["right"]:
        copy.wait_recv()
    right_s[...] = right_all[...].astype(f32).reshape(R * T * per, 128)
    for copy in arriving["left"]:
        copy.wait_recv()
    for b in range(B):
        left_s[b] = left_all[b // AX, b % AX].astype(f32).reshape(R * T * per, 128)
    same = iota((128, 128), 0) // J == iota((128, 128), 1) // J
    group = iota((M, 128), 1) // J

    def channel(c, carry):
        pick = pl.ds(c, R * T, stride=per)
        right = jnp.transpose(right_s[pick, :]).astype(bf16)
        for b in range(B):
            grid = dot(right, left_s[b, pick, :].astype(bf16), ((1,), (0,)))
            grid = jnp.where(same, grid, 0.0)
            folded = grid[:J]
            for q in range(1, Q):
                folded = folded + grid[q * J : (q + 1) * J]
            turn = 64
            while turn >= J:
                folded = folded + pltpu.roll(folded, turn, 1)
                turn //= 2
            packed = folded[:M]
            for g in range(1, Q):
                packed = jnp.where(group == g, folded[g * M : (g + 1) * M], packed)
            product_s[b, pl.ds(pl.multiple_of(c * M, M), M), :] = packed
        return carry

    lax.fori_loop(0, per, channel, 0)
    product_own[...] = product_s[...].astype(bf16)
    for a in range(1, AX):
        across[a].wait_recv()
        pass_on(a)
    to_res(4, "product", lambda to: ((product_own.at[to], product_all.at[p.r]),))
    product_all[p.r] = product_own[p.r]

    for copy in arriving["keys"]:
        copy.wait_recv()
    presence = joined([col_present[b // AX, b % AX] for b in range(B)], S * N)
    for g in range(A // N):
        keys = keys_all[:, :, :, g * N : (g + 1) * N, :F].reshape(B * S * N, F)
        values = keys_all[:, :, :, g * N : (g + 1) * N, F:].reshape(B * S * N, F)
        rows = jnp.concatenate([query[s * A + g * N : s * A + (g + 1) * N] for s in range(S)], axis=0)
        scores = dot(by_head(rows, H).astype(bf16), keys, ((1,), (1,))) * scale
        scores = scores + masked_fill_value * (presence[g : g + 1] - 1.0)
        scores = jnp.where(iota(scores.shape, 0) // H % N == iota(scores.shape, 1) % N, scores, -1e30)
        context = attend(scores, values, H)
        for s in range(S):
            context_s[s * A + g * N : s * A + (g + 1) * N, :] = context[s * N : (s + 1) * N]
    col_mix = (col_gate * context_s[...]).astype(bf16)
    after_col = after_row + dot(col_mix, col_exit[...], ((1,), (0,)))
    normed_third = normalize(after_col).astype(bf16)
    hidden = jnp.maximum(dot(normed_third, feed_first[...], ((1,), (0,))), 0.0).astype(bf16)
    alignment[...] = (after_col + dot(hidden, feed_second[...], ((1,), (0,)))).astype(bf16)

    for copy in arriving["product"]:
        copy.wait_recv()
    normed = normalize(product_all[...].astype(f32).reshape(C, M, 128), axis=0)
    final_s = left_s.at[0]
    final_s[: C * M, :] = normed.reshape(C * M, 128)
    for m in range(M):
        turned = jnp.transpose(final_s[pl.ds(m, C, stride=M), :]).astype(bf16)
        update = dot(turned, tri_exit[...], ((1,), (0,)))
        for g in range(Q):
            update_s[pl.ds(g * M + m, I, stride=J), :] = update[g * I : (g + 1) * I]
    pair[...] = (couple[...].astype(f32) + gate_s[...] * update_s[...]).astype(bf16)
    for copy in sent:
        copy.wait_send()


def on_device(
    sizes,
    homolog_features,
    couple_features,
    symbol_ids,
    entry_present,
    amino_present,
    symbol_lookup_matrix,
    horizontal_entry_matrix,
    couple_logit_matrix,
    horizontal_exit_matrix,
    vertical_entry_matrix,
    vertical_exit_matrix,
    feedforward_first_matrix,
    feedforward_second_matrix,
    trimul_entry_matrix,
    trimul_exit_matrix,
):
    R, BR, AX = sizes
    B = BR * AX
    S, A, F = homolog_features.shape
    H = couple_logit_matrix.shape[1]
    I, J, C = couple_features.shape
    per = C // R
    T = I * J // 128
    N = 16
    assert I == J and R == B and 128 % J == 0 and 128 % A == 0 and 128 % (S * N) == 0 and A % N == 0
    M = J // (128 // J)
    tokens = symbol_lookup_matrix.shape[0]
    indicator = (symbol_ids.reshape(-1, 1) == jnp.arange(tokens, dtype=jnp.int32)[None, :]).astype(bf16)
    here = entry_present.astype(f32)
    by_row = jnp.pad(jnp.tile(here, (1, 128 // A)), ((0, 8 - S), (0, 0)))
    by_col = jnp.tile(here.reshape(S, A // N, N).transpose(1, 0, 2).reshape(A // N, S * N), (1, 128 // (S * N)))
    by_col = jnp.pad(by_col, ((0, 8 - A // N), (0, 0)))
    present = jnp.stack([by_row, by_col])
    valid_res = amino_present.astype(f32)
    row_valid = lax.dynamic_slice_in_dim(valid_res, lax.axis_index("res") * I, I)
    col_valid = lax.dynamic_slice_in_dim(valid_res, lax.axis_index(("br", "aux")) * J, J)
    pair_valid = (row_valid[:, None] * col_valid[None, :]).reshape(1, I * J)
    pair_in = jnp.concatenate([trimul_entry_matrix[:, : 4 * C], couple_logit_matrix], axis=1).T
    operands = (
        homolog_features.reshape(S * A, F),
        couple_features.reshape(I * J, C),
        indicator,
        present,
        pair_valid,
        symbol_lookup_matrix,
        horizontal_entry_matrix,
        pair_in,
        horizontal_exit_matrix,
        vertical_entry_matrix,
        vertical_exit_matrix,
        feedforward_first_matrix,
        feedforward_second_matrix,
        trimul_entry_matrix[:, 4 * C :],
        trimul_exit_matrix,
    )
    vmem = pl.BlockSpec(memory_space=pltpu.VMEM)
    buffers = [
        ((S * A, F), bf16), ((H, I * J), f32), ((R, T, per, 128), bf16), ((R, T, per, 128), bf16),
        ((S, A, 2 * F), bf16), ((R, per * M, 128), bf16),
        ((R, S * A, F), bf16), ((R, 8, 128), f32), ((BR, AX, H, I * J), f32), ((BR, AX, 8, 128), f32),
        ((BR, AX, R, T, per, 128), bf16), ((R, T, per, 128), bf16), ((BR, AX, S, A, 2 * F), bf16),
        ((R, per * M, 128), bf16),
        ((S * A, F), f32), ((I * J, C), bf16), ((I * J, C), f32), ((I * H, B * J), f32),
        ((R, S * A, 2 * F), bf16), ((B, R * T * per, 128), f32), ((R * T * per, 128), f32),
        ((R, per * M, 128), f32), ((I * J, C), f32), ((S * A, F), f32),
    ]
    semaphores = [
        (5, R), (5, R), (2, B), (2, B), (R, AX), (R, AX), (R, AX, BR), (R, AX, BR),
        (AX,), (AX,), (AX, BR), (AX, BR),
    ]
    alignment, pair = pl.pallas_call(
        functools.partial(block_kernel, sizes, (S, A, F, H, I, J, C, per, T, N)),
        name="block",
        out_shape=[jax.ShapeDtypeStruct((S * A, F), bf16), jax.ShapeDtypeStruct((I * J, C), bf16)],
        in_specs=[vmem] * len(operands),
        out_specs=[vmem] * 2,
        scratch_shapes=[pltpu.VMEM(*b) for b in buffers] + [pltpu.SemaphoreType.DMA(s) for s in semaphores],
        compiler_params=pltpu.CompilerParams(
            collective_id=1, has_side_effects=True, vmem_limit_bytes=60 * 1024 * 1024
        ),
    )(*operands)
    return (alignment.reshape(S, A, F), pair.reshape(I, J, C))


def solution(mesh):
    sizes = (mesh.shape["res"], mesh.shape["br"], mesh.shape["aux"])
    return jax.shard_map(
        functools.partial(on_device, sizes),
        mesh=mesh,
        in_specs=(
            P(("grp", "br", "aux"), "res", None),
            P(("grp", "res"), ("br", "aux"), None),
            P(("grp", "br", "aux"), "res"),
            P(("grp", "br", "aux"), "res"),
            P("grp"),
        )
        + (P(),) * 10,
        out_specs=(P(("grp", "br", "aux"), "res", None), P(("grp", "res"), ("br", "aux"), None)),
        check_vma=False,
    )
```

time: 83.3 us -> 58.3 us (0.70)
  matrix products: 16 us -> 0 us
  Pallas kernels: 36.2 us -> 46.7 us
  other arithmetic: 13.2 us -> 3.37 us
  local copies, waits for them, and re-layouts: 16 us -> 7.25 us
    dot_general x16 -> x0, matrix products: 16 us -> none  [the longest x11 8.77 us: dot(): lax.dot_general(a, b, (contract, ((), ())), preferred_element_type=f32)]
    reshape x15 -> x1, local copies, waits for them, and re-layouts: 12.2 us -> 0.08 us  [on_device(): here.reshape(S, A // N, N).transpose(1, 0, 2).reshape(A // N, S * N)]
    pallas_call x2 -> x1, Pallas kernels: 36.2 us -> 46.7 us  [on_device(): pl.pallas_call(functools.partial(block_kernel, sizes, (S, A, F, H, I, J,...]
    reduce_sum x9 -> x0, other arithmetic: 6.83 us -> none  [the longest x5 2.9 us: normalize(): variance = jnp.mean(centred * centred, axis=axis, keepdims=True)]
    convert_element_type x6 -> x2, other arithmetic: 5.48 us -> 1.38 us  [the longest x1 0.7 us: on_device(): (symbol_ids.reshape(-1, 1) == jnp.arange(tokens, dtype=jnp.int32)[None, :...]
    unnamed x42 -> x7, local copies, waits for them, and re-layouts: 0.78 us -> 3.82 us
    slice x8 -> x3, local copies, waits for them, and re-layouts: 2.06 us -> 1.52 us  [the longest x2 0.9 us: on_device(): trimul_entry_matrix[:, :4 * C]]
where the time goes in v2:
time: 58.3 us; the launch traced here: 58 us
  Pallas kernels  46.7 us (80%)
  local copies, waits for them, and re-layouts  7.25 us (12%)
  other arithmetic  3.37 us (6%)
  between operations  0.67 us (1%)
    pallas_call x1, Pallas kernels, on_device(): pl.pallas_call(functools.partial(block_kernel, sizes, (S, A, F, H, I, J,...  46.7 us
    unnamed x7, local copies, waits for them, and re-layouts  3.82 us

profile of v2, /device:TPU:0, one launch (start us, length us, event | category | flops | bytes accessed | tf_op | source)
XLA Modules:
  0.0 58.0 jit_solution(6741222701535252868)
XLA Ops:
  0.6 0.0 copy-start
  0.7 0.8 %eq.15 = s32[128]{0:T(128)S(1)} reshape(s32[4,32]{1,0:T(4,128)} %param.17) | data formatting | bytes 1024 | tf_op jit(solution)/shard_map/eq | solution.py:366
  1.4 0.7 %convert_element_type.15 = f32[128]{0:T(128)S(1)} convert(s32[128]{0:T(128)} %param.19) | non-fusion elementwise | flops 128 | bytes 1024 | tf_op jit(solution)/shard_map/convert_element_type | solution.py:372
  2.1 0.1 fusion.1
  2.2 0.7 %convert_element_type.14 = f32[4,32]{1,0:T(4,128)S(1)} convert(s32[4,32]{1,0:T(4,128)} %param.18) | non-fusion elementwise | flops 128 | bytes 1024 | tf_op jit(solution)/shard_map/convert_element_type | solution.py:367
  2.9 0.1 reshape.56
  3.0 0.1 tile.21
  3.1 0.1 tile.23
  3.1 0.1 tile.20
  3.2 0.6 %pad_maximum_fusion.present = f32[2,8,128]{2,1,0:T(8,128)} fusion(f32[1,8,128]{2,1,0:T(8,128)S(1)} %get-tuple-element.8, f32[1,8,128]{2,1,0:T(8,128)S(1)} %get-tuple-element.9), kind=kLoop, calls=%fused_computation.3 | loop fusion | flops 2048 | bytes 16384 | tf_op jit(solution)/shard_map/stack | solution.py:371
  3.8 0.1 broadcast_multiply_fusion
  3.9 0.7 %mul.38.pair_valid = f32[1,1024]{1,0:T(1,128)} reshape(f32[32,32]{1,0:T(8,128)S(1)} %broadcast_multiply_fusion) | data formatting | bytes 8192 | tf_op jit(solution)/shard_map/mul | solution.py:375
  4.6 0.7 %fusion.indicator = bf16[128,23]{1,0:T(8,128)(2,1)} fusion(s32[128]{0:T(128)S(1)} %eq.15), kind=kLoop, calls=%fused_computation.2 | loop fusion | flops 5888 | bytes 6400 | tf_op jit(solution)/shard_map/convert_element_type | solution.py:366
  5.3 0.0 copy-done
  5.3 0.6 %slice.7.gate_in = bf16[128,128]{1,0:T(8,128)(2,1)} slice(bf16[128,640]{1,0:T(8,128)(2,1)S(1)} %copy-done), slice={[0:128], [512:640]} | slice | bytes 65536 | tf_op jit(solution)/shard_map/slice | solution.py:391
  5.9 0.0 slice-start
  5.9 0.9 %slice-done = bf16[128,512]{1,0:T(8,128)(2,1)S(1)} async-done(((bf16[128,640]{1,0:T(8,128)(2,1)}), bf16[128,512]{1,0:T(8,128)(2,1)S(1)}, s32[]{:S(2)}) %slice-start) | async-done | bytes 131096 | tf_op jit(solution)/shard_map/slice | solution.py:376
  6.8 0.0 copy-start.1
  6.8 0.1 copy.19
  6.9 0.6 copy-done.1
  7.5 0.7 %maximum_bitcast_fusion.pair_in = bf16[520,128]{1,0:T(8,128)(2,1)} fusion(bf16[128,8]{0,1:T(8,128)(2,1)S(1)} %copy-done.1, bf16[128,512]{0,1:T(8,128)(2,1)S(1)} %copy.19), kind=kLoop, calls=%fused_computation | loop fusion | flops 266240 | bytes 266240 | tf_op jit(solution)/shard_map/transpose | solution.py:376
  8.1 46.7 %block.1 = (bf16[128,256]{1,0:T(8,128)(2,1)}, bf16[1024,128]{1,0:T(8,128)(2,1)}) custom-call(bf16[128,256]{1,0:T(8,128)(2,1)} %bitcast.13, bf16[1024,128]{1,0:T(8,128)(2,1)} %bitcast.11, bf16[128,23]{1,0:T(8,128)(2,1)} %fusion.indicator, f32[2,8,128]{2,1,0:T(8,128)} %pad_maximum_fusion.present, f32[1,1024]{1,0:T(1,128)} %mul.38.pair_valid, ...), custom_call_target="tpu_custom_call" | custom-call | tf_op jit(solution)/shard_map/block/pallas_call | solution.py:409
  54.9 1.5 %copy.22 = bf16[4,32,256]{2,1,0:T(8,128)(2,1)} copy(bf16[4,32,256]{2,1,0:T(8,128)(2,1)} %bitcast.14) | data formatting | bytes 131072
  56.3 1.7 %copy.23 = bf16[32,32,128]{2,1,0:T(8,128)(2,1)} copy(bf16[32,32,128]{2,1,0:T(8,128)(2,1)} %bitcast.12) | data formatting | bytes 524288
  (4 shorter events, 0.0 us)
Async XLA Ops:
  0.6 4.7 %copy-start = (bf16[128,640]{1,0:T(8,128)(2,1)S(1)}, bf16[128,640]{1,0:T(8,128)(2,1)}, u32[]{:S(2)}) copy-start(bf16[128,640]{1,0:T(8,128)(2,1)} %param.28) | copy-start | bytes 491524
  5.9 0.9 %slice-start = ((bf16[128,640]{1,0:T(8,128)(2,1)}), bf16[128,512]{1,0:T(8,128)(2,1)S(1)}, s32[]{:S(2)}) async-start(bf16[128,640]{1,0:T(8,128)(2,1)} %param.28), calls=%async_computation | async-start | bytes 262144 | tf_op jit(solution)/shard_map/slice | solution.py:376
  6.8 0.7 %copy-start.1 = (bf16[128,8]{0,1:T(8,128)(2,1)S(1)}, bf16[128,8]{0,1:T(8,128)(2,1)}, u32[]{:S(2)}) copy-start(bf16[128,8]{0,1:T(8,128)(2,1)} %param.22) | copy-start | bytes 6148

commit v3 on v2

--- a/solution.py
+++ b/solution.py
@@ -109,14 +109,15 @@
 
 def block_kernel(
     sizes, dims,
-    homolog, couple, indicator, present, pair_valid, table, row_in, pair_in, row_exit, col_in, col_exit,
-    feed_first, feed_second, gate_in, tri_exit,
+    homolog, couple, symbols, entries, amino, table, logit, tri_in, tri_exit,
+    row_in_far, row_exit_far, col_in_far, col_exit_far, feed_first_far, feed_second_far,
     alignment, pair,
     rows_own, bias_own, left_own, right_own, keys_own, product_own,
     rows_all, row_present, bias_all, col_present, left_all, right_all, keys_all, product_all,
+    row_in, row_exit, col_in, col_exit, feed_first, feed_second, present,
     embedded_s, pair_norm_s, gate_s, bias_s, key_value_s, left_s, right_s, product_s, update_s, context_s,
     res_send, res_recv, grp_send, grp_recv, aux_send, aux_recv, br_send, br_recv,
-    across_send, across_recv, over_send, over_recv,
+    across_send, across_recv, over_send, over_recv, weight_sem,
 ):
     p = Peers(sizes)
     R, BR, AX = sizes
@@ -126,21 +127,50 @@
     Q = 128 // J
     M = J // Q
     p.greet()
+    weights = []
+    for n, (far, near) in enumerate(
+        (
+            (row_in_far, row_in),
+            (row_exit_far, row_exit),
+            (col_in_far, col_in),
+            (col_exit_far, col_exit),
+            (feed_first_far, feed_first),
+            (feed_second_far, feed_second),
+        )
+    ):
+        weights.append(pltpu.make_async_copy(far, near, weight_sem.at[n]))
+        weights[n].start()
     sent = []
     arriving = {"rows": [], "bias": [], "right": [], "left": [], "keys": [], "product": []}
 
     pair_norm = normalize(couple[...]).astype(bf16)
     pair_norm_s[...] = pair_norm
+    alive = jnp.broadcast_to(amino[...].astype(f32), (8, amino.shape[1])).astype(bf16)
+    residue = iota((amino.shape[1], I * J), 0)
+    flat = iota((amino.shape[1], I * J), 1)
+    row_pick = (residue == p.r * I + flat // J).astype(f32).astype(bf16)
+    col_pick = (residue == (p.b * AX + p.x) * J + flat % J).astype(f32).astype(bf16)
+    pair_valid = (dot(alive, row_pick, ((1,), (0,))) * dot(alive, col_pick, ((1,), (0,))))[:1]
+    turned_in = [jnp.transpose(tri_in[:, n * C : (n + 1) * C].astype(f32)).astype(bf16) for n in range(4)]
     for side, own in ((0, left_own), (1, right_own)):
-        first = 2 * side * C
-        value = dot(pair_in[first : first + C, :], pair_norm, ((1,), (1,)))
-        sigma = jax.nn.sigmoid(dot(pair_in[first + C : first + 2 * C, :], pair_norm, ((1,), (1,))))
-        value = sigma * value * pair_valid[...]
+        value = dot(turned_in[2 * side], pair_norm, ((1,), (1,)))
+        sigma = jax.nn.sigmoid(dot(turned_in[2 * side + 1], pair_norm, ((1,), (1,))))
+        value = sigma * value * pair_valid
         for n in range(R):
             for t in range(T):
                 own[n, t] = value[n * per : (n + 1) * per, t * 128 : (t + 1) * 128].astype(bf16)
-    bias_own[...] = dot(pair_in[4 * C :, :], pair_norm, ((1,), (1,)))
-    embedded = homolog[...].astype(f32) + dot(indicator[...], table[...], ((1,), (0,)))
+    bias_own[...] = dot(jnp.transpose(logit[...].astype(f32)).astype(bf16), pair_norm, ((1,), (1,)))
+    here = entries[...].astype(f32)
+    present[...] = jnp.zeros_like(present)
+    present[0, :S, :] = jnp.concatenate([here] * (128 // A), axis=1)
+    for g in range(A // N):
+        pieces = [here[s : s + 1, g * N : (g + 1) * N] for s in range(S)]
+        present[1, g : g + 1, :] = jnp.concatenate(pieces * (128 // (S * N)), axis=1)
+    tokens = table.shape[0]
+    for s in range(S):
+        chosen = (iota((tokens, A), 0) == symbols[s : s + 1, :]).astype(f32)
+        context_s[s * A : (s + 1) * A, :] = dot(jnp.transpose(chosen).astype(bf16), table[...], ((1,), (0,)))
+    embedded = homolog[...].astype(f32) + context_s[...]
     embedded_s[...] = embedded
     normed_first = normalize(embedded).astype(bf16)
     rows_own[...] = normed_first
@@ -201,9 +231,10 @@
     left_all[p.b, p.x, p.r] = left_own[p.r]
     right_all[p.r] = right_own[p.r]
 
+    weights[0].wait()
     query = dot(normed_first, row_in[:, :F], ((1,), (0,))).astype(bf16).astype(f32)
     row_gate = jax.nn.sigmoid(dot(normed_first, row_in[:, 3 * F :], ((1,), (0,))))
-    gate_s[...] = jax.nn.sigmoid(dot(pair_norm, gate_in[...], ((1,), (0,))))
+    gate_s[...] = jax.nn.sigmoid(dot(pair_norm, tri_in[:, 4 * C :], ((1,), (0,))))
 
     for d in range(1, R):
         lefts[d].wait_recv()
@@ -239,6 +270,8 @@
         scores = dot(by_head(query[mine], H).astype(bf16), keys, ((1,), (1,))) * scale
         scores = scores + bias_s[...] + masked_fill_value * (presence[s : s + 1] - 1.0)
         context_s[mine, :] = attend(scores, values, H)
+    weights[1].wait()
+    weights[2].wait()
     row_mix = (row_gate * context_s[...]).astype(bf16)
     after_row = embedded_s[...] + dot(row_mix, row_exit[...], ((1,), (0,)))
     normed_second = normalize(after_row).astype(bf16)
@@ -270,29 +303,33 @@
         copy.wait_recv()
     for b in range(B):
         left_s[b] = left_all[b // AX, b % AX].astype(f32).reshape(R * T * per, 128)
-    same = iota((128, 128), 0) // J == iota((128, 128), 1) // J
-    group = iota((M, 128), 1) // J
+    wide = iota((J, 128), 1) // J
+    lane = iota((M, 128), 1)
 
     def channel(c, carry):
         pick = pl.ds(c, R * T, stride=per)
         right = jnp.transpose(right_s[pick, :]).astype(bf16)
+        lefts = jnp.concatenate([left_s[b, pick, :].astype(bf16) for b in range(B)], axis=1)
+        grid = dot(right, lefts, ((1,), (0,)))
         for b in range(B):
-            grid = dot(right, left_s[b, pick, :].astype(bf16), ((1,), (0,)))
-            grid = jnp.where(same, grid, 0.0)
-            folded = grid[:J]
+            tile = grid[:, b * 128 : (b + 1) * 128]
+            folded = tile[:J]
             for q in range(1, Q):
-                folded = folded + grid[q * J : (q + 1) * J]
-            turn = 64
-            while turn >= J:
-                folded = folded + pltpu.roll(folded, turn, 1)
-                turn //= 2
-            packed = folded[:M]
-            for g in range(1, Q):
-                packed = jnp.where(group == g, folded[g * M : (g + 1) * M], packed)
-            product_s[b, pl.ds(pl.multiple_of(c * M, M), M), :] = packed
+                folded = jnp.where(wide == q, tile[q * J : (q + 1) * J], folded)
+            pieces = [folded[g * M : (g + 1) * M] for g in range(Q)]
+            turn = J
+            while turn < 128:
+                low = (lane & turn) == 0
+                pieces = [
+                    jnp.where(low, pieces[k], pieces[k + 1])
+                    + pltpu.roll(jnp.where(low, pieces[k + 1], pieces[k]), turn, 1)
+                    for k in range(0, len(pieces), 2)
+                ]
+                turn *= 2
+            product_s[b, pl.ds(pl.multiple_of(c * M, M), M), :] = pieces[0]
         return carry
 
-    lax.fori_loop(0, per, channel, 0)
+    lax.fori_loop(0, per, channel, 0, unroll=4)
     product_own[...] = product_s[...].astype(bf16)
     for a in range(1, AX):
         across[a].wait_recv()
@@ -313,6 +350,8 @@
         context = attend(scores, values, H)
         for s in range(S):
             context_s[s * A + g * N : s * A + (g + 1) * N, :] = context[s * N : (s + 1) * N]
+    for n in (3, 4, 5):
+        weights[n].wait()
     col_mix = (col_gate * context_s[...]).astype(bf16)
     after_col = after_row + dot(col_mix, col_exit[...], ((1,), (0,)))
     normed_third = normalize(after_col).astype(bf16)
@@ -362,34 +401,24 @@
     N = 16
     assert I == J and R == B and 128 % J == 0 and 128 % A == 0 and 128 % (S * N) == 0 and A % N == 0
     M = J // (128 // J)
-    tokens = symbol_lookup_matrix.shape[0]
-    indicator = (symbol_ids.reshape(-1, 1) == jnp.arange(tokens, dtype=jnp.int32)[None, :]).astype(bf16)
-    here = entry_present.astype(f32)
-    by_row = jnp.pad(jnp.tile(here, (1, 128 // A)), ((0, 8 - S), (0, 0)))
-    by_col = jnp.tile(here.reshape(S, A // N, N).transpose(1, 0, 2).reshape(A // N, S * N), (1, 128 // (S * N)))
-    by_col = jnp.pad(by_col, ((0, 8 - A // N), (0, 0)))
-    present = jnp.stack([by_row, by_col])
-    valid_res = amino_present.astype(f32)
-    row_valid = lax.dynamic_slice_in_dim(valid_res, lax.axis_index("res") * I, I)
-    col_valid = lax.dynamic_slice_in_dim(valid_res, lax.axis_index(("br", "aux")) * J, J)
-    pair_valid = (row_valid[:, None] * col_valid[None, :]).reshape(1, I * J)
-    pair_in = jnp.concatenate([trimul_entry_matrix[:, : 4 * C], couple_logit_matrix], axis=1).T
-    operands = (
+    near = (
         homolog_features.reshape(S * A, F),
         couple_features.reshape(I * J, C),
-        indicator,
-        present,
-        pair_valid,
+        symbol_ids,
+        entry_present,
+        amino_present.reshape(1, -1),
         symbol_lookup_matrix,
+        couple_logit_matrix,
+        trimul_entry_matrix,
+        trimul_exit_matrix,
+    )
+    far = (
         horizontal_entry_matrix,
-        pair_in,
         horizontal_exit_matrix,
         vertical_entry_matrix,
         vertical_exit_matrix,
         feedforward_first_matrix,
         feedforward_second_matrix,
-        trimul_entry_matrix[:, 4 * C :],
-        trimul_exit_matrix,
     )
     vmem = pl.BlockSpec(memory_space=pltpu.VMEM)
     buffers = [
@@ -398,25 +427,26 @@
         ((R, S * A, F), bf16), ((R, 8, 128), f32), ((BR, AX, H, I * J), f32), ((BR, AX, 8, 128), f32),
         ((BR, AX, R, T, per, 128), bf16), ((R, T, per, 128), bf16), ((BR, AX, S, A, 2 * F), bf16),
         ((R, per * M, 128), bf16),
+        *[(weight.shape, bf16) for weight in far], ((2, 8, 128), f32),
         ((S * A, F), f32), ((I * J, C), bf16), ((I * J, C), f32), ((I * H, B * J), f32),
         ((R, S * A, 2 * F), bf16), ((B, R * T * per, 128), f32), ((R * T * per, 128), f32),
         ((R, per * M, 128), f32), ((I * J, C), f32), ((S * A, F), f32),
     ]
     semaphores = [
         (5, R), (5, R), (2, B), (2, B), (R, AX), (R, AX), (R, AX, BR), (R, AX, BR),
-        (AX,), (AX,), (AX, BR), (AX, BR),
+        (AX,), (AX,), (AX, BR), (AX, BR), (len(far),),
     ]
     alignment, pair = pl.pallas_call(
         functools.partial(block_kernel, sizes, (S, A, F, H, I, J, C, per, T, N)),
         name="block",
         out_shape=[jax.ShapeDtypeStruct((S * A, F), bf16), jax.ShapeDtypeStruct((I * J, C), bf16)],
-        in_specs=[vmem] * len(operands),
+        in_specs=[vmem] * len(near) + [pl.BlockSpec(memory_space=pl.ANY)] * len(far),
         out_specs=[vmem] * 2,
         scratch_shapes=[pltpu.VMEM(*b) for b in buffers] + [pltpu.SemaphoreType.DMA(s) for s in semaphores],
         compiler_params=pltpu.CompilerParams(
             collective_id=1, has_side_effects=True, vmem_limit_bytes=60 * 1024 * 1024
         ),
-    )(*operands)
+    )(*near, *far)
     return (alignment.reshape(S, A, F), pair.reshape(I, J, C))
 
 

time: 58.3 us -> 42.4 us (0.73)
  Pallas kernels: 46.7 us -> 37 us
  other arithmetic: 3.37 us -> 0 us
  local copies, waits for them, and re-layouts: 7.25 us -> 4.54 us
    pallas_call x1, Pallas kernels: 46.7 us -> 37 us  [on_device(): pl.pallas_call(functools.partial(block_kernel, sizes, (S, A, F, H, I, J,...]
    convert_element_type x3 -> x0, other arithmetic: 2.04 us -> none  [the longest x1 0.7 us: on_device(): (symbol_ids.reshape(-1, 1) == jnp.arange(tokens, dtype=jnp.int32)[None, :...]
    slice x3 -> x0, local copies, waits for them, and re-layouts: 1.52 us -> none  [the longest x2 0.9 us: on_device(): trimul_entry_matrix[:, :4 * C]]
    eq x1 -> x0, local copies, waits for them, and re-layouts: 0.8 us -> none  [on_device(): symbol_ids.reshape(-1, 1) == jnp.arange(tokens, dtype=jnp.int32)[None, :]]
    unnamed x7 -> x5, local copies, waits for them, and re-layouts: 3.82 us -> 4.54 us
    mul x1 -> x0, local copies, waits for them, and re-layouts: 0.68 us -> none  [on_device(): pair_valid = (row_valid[:, None] * col_valid[None, :]).reshape(1, I * J)]
    transpose x1 -> x0, other arithmetic: 0.67 us -> none  [on_device(): jnp.concatenate([trimul_entry_matrix[:, :4 * C], couple_logit_matrix], ax...]
    another operation x1 -> x0, other arithmetic: 0.6 us -> none  [on_device(): present = jnp.stack([by_row, by_col])]
where the time goes in v3:
time: 42.4 us; the launch traced here: 42.2 us
  Pallas kernels  37 us (87%)
  local copies, waits for them, and re-layouts  4.54 us (11%)
  between operations  0.65 us (2%)
    pallas_call x1, Pallas kernels, on_device(): pl.pallas_call(functools.partial(block_kernel, sizes, (S, A, F, H, I, J,...  37 us
    unnamed x5, local copies, waits for them, and re-layouts  4.54 us

profile of v3, /device:TPU:0, one launch (start us, length us, event | category | flops | bytes accessed | tf_op | source)
XLA Modules:
  0.0 42.2 jit_solution(14047017211953088407)
XLA Ops:
  0.6 0.0 copy-start
  0.6 0.7 %copy-done = bf16[128,8]{0,1:T(8,128)(2,1)S(1)} copy-done((bf16[128,8]{0,1:T(8,128)(2,1)S(1)}, bf16[128,8]{0,1:T(8,128)(2,1)}, u32[]{:S(2)}) %copy-start) | copy-done | bytes 2072
  1.3 0.7 %copy.17.logit = bf16[128,8]{1,0:T(8,128)(2,1)} copy(bf16[128,8]{0,1:T(8,128)(2,1)S(1)} %copy-done) | data formatting | bytes 4096 | tf_op args[7]
  2.0 37.0 %block.1 = (bf16[128,256]{1,0:T(8,128)(2,1)}, bf16[1024,128]{1,0:T(8,128)(2,1)}) custom-call(bf16[128,256]{1,0:T(8,128)(2,1)} %bitcast.7, bf16[1024,128]{1,0:T(8,128)(2,1)} %bitcast.5, s32[4,32]{1,0:T(4,128)} %symbols.1, s32[4,32]{1,0:T(4,128)} %entries.1, s32[1,128]{1,0:T(1,128)} %bitcast.9, bf16[23,256]{1,0:T(8,128)(2,1)} %table.1, ...), custom_call_target="tpu_custom_call" | custom-call | tf_op jit(solution)/shard_map/block/pallas_call | solution.py:439
  39.1 1.5 %copy.20 = bf16[4,32,256]{2,1,0:T(8,128)(2,1)} copy(bf16[4,32,256]{2,1,0:T(8,128)(2,1)} %bitcast.8) | data formatting | bytes 131072
  40.5 1.7 %copy.21 = bf16[32,32,128]{2,1,0:T(8,128)(2,1)} copy(bf16[32,32,128]{2,1,0:T(8,128)(2,1)} %bitcast.6) | data formatting | bytes 524288
Async XLA Ops:
  0.6 0.7 %copy-start = (bf16[128,8]{0,1:T(8,128)(2,1)S(1)}, bf16[128,8]{0,1:T(8,128)(2,1)}, u32[]{:S(2)}) copy-start(bf16[128,8]{0,1:T(8,128)(2,1)} %param.22) | copy-start | bytes 6148

commit v4 on v3

--- a/solution.py
+++ b/solution.py
@@ -152,13 +152,14 @@
     col_pick = (residue == (p.b * AX + p.x) * J + flat % J).astype(f32).astype(bf16)
     pair_valid = (dot(alive, row_pick, ((1,), (0,))) * dot(alive, col_pick, ((1,), (0,))))[:1]
     turned_in = [jnp.transpose(tri_in[:, n * C : (n + 1) * C].astype(f32)).astype(bf16) for n in range(4)]
-    for side, own in ((0, left_own), (1, right_own)):
+    def project(side, own):
         value = dot(turned_in[2 * side], pair_norm, ((1,), (1,)))
         sigma = jax.nn.sigmoid(dot(turned_in[2 * side + 1], pair_norm, ((1,), (1,))))
         value = sigma * value * pair_valid
         for n in range(R):
             for t in range(T):
                 own[n, t] = value[n * per : (n + 1) * per, t * 128 : (t + 1) * 128].astype(bf16)
+    project(0, left_own)
     bias_own[...] = dot(jnp.transpose(logit[...].astype(f32)).astype(bf16), pair_norm, ((1,), (1,)))
     here = entries[...].astype(f32)
     present[...] = jnp.zeros_like(present)
@@ -166,16 +167,8 @@
     for g in range(A // N):
         pieces = [here[s : s + 1, g * N : (g + 1) * N] for s in range(S)]
         present[1, g : g + 1, :] = jnp.concatenate(pieces * (128 // (S * N)), axis=1)
-    tokens = table.shape[0]
-    for s in range(S):
-        chosen = (iota((tokens, A), 0) == symbols[s : s + 1, :]).astype(f32)
-        context_s[s * A : (s + 1) * A, :] = dot(jnp.transpose(chosen).astype(bf16), table[...], ((1,), (0,)))
-    embedded = homolog[...].astype(f32) + context_s[...]
-    embedded_s[...] = embedded
-    normed_first = normalize(embedded).astype(bf16)
-    rows_own[...] = normed_first
-
     p.met()
+
 
     def relay(d, a):
         origin = (p.b, p.aux_back(a), p.res_back(d))
@@ -216,6 +209,17 @@
         )
         sent.append(lefts[d])
     spreads = {0: spread(0)}
+    project(1, right_own)
+    tokens = table.shape[0]
+    for s in range(S):
+        chosen = (iota((tokens, A), 0) == symbols[s : s + 1, :]).astype(f32)
+        context_s[s * A : (s + 1) * A, :] = dot(jnp.transpose(chosen).astype(bf16), table[...], ((1,), (0,)))
+    embedded = homolog[...].astype(f32) + context_s[...]
+    embedded_s[...] = embedded
+    normed_first = normalize(embedded).astype(bf16)
+    rows_own[...] = normed_first
+
+    to_res(3, "right", lambda to: ((right_own.at[to], right_all.at[p.r]),))
     to_res(1, "rows", lambda to: ((rows_own, rows_all.at[p.r]), (present.at[0], row_present.at[p.r])))
     for n, (bo, a) in enumerate(p.group()):
         to = {"br": p.br(bo), "aux": p.aux(a)}
@@ -223,7 +227,6 @@
             copy = remote(src, dst.at[p.b, p.x], grp_send.at[m, n], grp_recv.at[m, n], to)
             sent.append(copy)
             arriving["bias"].append(copy)
-    to_res(3, "right", lambda to: ((right_own.at[to], right_all.at[p.r]),))
     rows_all[p.r] = rows_own[...]
     row_present[p.r] = present[0]
     bias_all[p.b, p.x] = bias_own[...]
@@ -254,47 +257,6 @@
         for a in range(1, AX):
             spreads[d][a].wait_recv()
             relay(d, a)
-
-    for copy in arriving["rows"]:
-        copy.wait_recv()
-    key_value_s[...] = (
-        dot(rows_all[...].reshape(R * S * A, F), row_in[:, F : 3 * F], ((1,), (0,)))
-        .astype(bf16)
-        .reshape(R, S * A, 2 * F)
-    )
-    presence = joined([row_present[n] for n in range(R)], A)
-    for s in range(S):
-        mine = slice(s * A, (s + 1) * A)
-        keys = key_value_s[:, mine, :F].reshape(R * A, F)
-        values = key_value_s[:, mine, F:].reshape(R * A, F)
-        scores = dot(by_head(query[mine], H).astype(bf16), keys, ((1,), (1,))) * scale
-        scores = scores + bias_s[...] + masked_fill_value * (presence[s : s + 1] - 1.0)
-        context_s[mine, :] = attend(scores, values, H)
-    weights[1].wait()
-    weights[2].wait()
-    row_mix = (row_gate * context_s[...]).astype(bf16)
-    after_row = embedded_s[...] + dot(row_mix, row_exit[...], ((1,), (0,)))
-    normed_second = normalize(after_row).astype(bf16)
-    keys_own[...] = dot(normed_second, col_in[:, F : 3 * F], ((1,), (0,))).astype(bf16).reshape(S, A, 2 * F)
-    query = dot(normed_second, col_in[:, :F], ((1,), (0,))).astype(bf16).astype(f32)
-    col_gate = jax.nn.sigmoid(dot(normed_second, col_in[:, 3 * F :], ((1,), (0,))))
-
-    def pass_on(a):
-        origin = (p.b, p.aux_back(a))
-        src = keys_own if a == 0 else keys_all.at[origin]
-        for bo in range(1, BR):
-            copy = remote(src, keys_all.at[origin], over_send.at[a, bo], over_recv.at[a, bo], {"br": p.br(bo)})
-            sent.append(copy)
-            arriving["keys"].append(copy)
-
-    across = {}
-    for a in range(1, AX):
-        across[a] = remote(
-            keys_own, keys_all.at[p.b, p.x], across_send.at[a], across_recv.at[a], {"aux": p.aux(a)}
-        )
-        sent.append(across[a])
-    pass_on(0)
-    keys_all[p.b, p.x] = keys_own[...]
 
     for copy in arriving["right"]:
         copy.wait_recv()
@@ -331,12 +293,53 @@
 
     lax.fori_loop(0, per, channel, 0, unroll=4)
     product_own[...] = product_s[...].astype(bf16)
+    to_res(4, "product", lambda to: ((product_own.at[to], product_all.at[p.r]),))
+    product_all[p.r] = product_own[p.r]
+
+    for copy in arriving["rows"]:
+        copy.wait_recv()
+    key_value_s[...] = (
+        dot(rows_all[...].reshape(R * S * A, F), row_in[:, F : 3 * F], ((1,), (0,)))
+        .astype(bf16)
+        .reshape(R, S * A, 2 * F)
+    )
+    presence = joined([row_present[n] for n in range(R)], A)
+    for s in range(S):
+        mine = slice(s * A, (s + 1) * A)
+        keys = key_value_s[:, mine, :F].reshape(R * A, F)
+        values = key_value_s[:, mine, F:].reshape(R * A, F)
+        scores = dot(by_head(query[mine], H).astype(bf16), keys, ((1,), (1,))) * scale
+        scores = scores + bias_s[...] + masked_fill_value * (presence[s : s + 1] - 1.0)
+        context_s[mine, :] = attend(scores, values, H)
+    weights[1].wait()
+    weights[2].wait()
+    row_mix = (row_gate * context_s[...]).astype(bf16)
+    after_row = embedded_s[...] + dot(row_mix, row_exit[...], ((1,), (0,)))
+    normed_second = normalize(after_row).astype(bf16)
+    keys_own[...] = dot(normed_second, col_in[:, F : 3 * F], ((1,), (0,))).astype(bf16).reshape(S, A, 2 * F)
+    query = dot(normed_second, col_in[:, :F], ((1,), (0,))).astype(bf16).astype(f32)
+    col_gate = jax.nn.sigmoid(dot(normed_second, col_in[:, 3 * F :], ((1,), (0,))))
+
+    def pass_on(a):
+        origin = (p.b, p.aux_back(a))
+        src = keys_own if a == 0 else keys_all.at[origin]
+        for bo in range(1, BR):
+            copy = remote(src, keys_all.at[origin], over_send.at[a, bo], over_recv.at[a, bo], {"br": p.br(bo)})
+            sent.append(copy)
+            arriving["keys"].append(copy)
+
+    across = {}
+    for a in range(1, AX):
+        across[a] = remote(
+            keys_own, keys_all.at[p.b, p.x], across_send.at[a], across_recv.at[a], {"aux": p.aux(a)}
+        )
+        sent.append(across[a])
+    pass_on(0)
+    keys_all[p.b, p.x] = keys_own[...]
+
     for a in range(1, AX):
         across[a].wait_recv()
         pass_on(a)
-    to_res(4, "product", lambda to: ((product_own.at[to], product_all.at[p.r]),))
-    product_all[p.r] = product_own[p.r]
-
     for copy in arriving["keys"]:
         copy.wait_recv()
     presence = joined([col_present[b // AX, b % AX] for b in range(B)], S * N)
@@ -356,7 +359,7 @@
     after_col = after_row + dot(col_mix, col_exit[...], ((1,), (0,)))
     normed_third = normalize(after_col).astype(bf16)
     hidden = jnp.maximum(dot(normed_third, feed_first[...], ((1,), (0,))), 0.0).astype(bf16)
-    alignment[...] = (after_col + dot(hidden, feed_second[...], ((1,), (0,)))).astype(bf16)
+    alignment[...] = after_col + dot(hidden, feed_second[...], ((1,), (0,)))
 
     for copy in arriving["product"]:
         copy.wait_recv()
@@ -368,7 +371,7 @@
         update = dot(turned, tri_exit[...], ((1,), (0,)))
         for g in range(Q):
             update_s[pl.ds(g * M + m, I, stride=J), :] = update[g * I : (g + 1) * I]
-    pair[...] = (couple[...].astype(f32) + gate_s[...] * update_s[...]).astype(bf16)
+    pair[...] = couple[...].astype(f32) + gate_s[...] * update_s[...]
     for copy in sent:
         copy.wait_send()
 
@@ -439,7 +442,7 @@
     alignment, pair = pl.pallas_call(
         functools.partial(block_kernel, sizes, (S, A, F, H, I, J, C, per, T, N)),
         name="block",
-        out_shape=[jax.ShapeDtypeStruct((S * A, F), bf16), jax.ShapeDtypeStruct((I * J, C), bf16)],
+        out_shape=[jax.ShapeDtypeStruct((S * A, F), f32), jax.ShapeDtypeStruct((I * J, C), f32)],
         in_specs=[vmem] * len(near) + [pl.BlockSpec(memory_space=pl.ANY)] * len(far),
         out_specs=[vmem] * 2,
         scratch_shapes=[pltpu.VMEM(*b) for b in buffers] + [pltpu.SemaphoreType.DMA(s) for s in semaphores],
@@ -447,7 +450,7 @@
             collective_id=1, has_side_effects=True, vmem_limit_bytes=60 * 1024 * 1024
         ),
     )(*near, *far)
-    return (alignment.reshape(S, A, F), pair.reshape(I, J, C))
+    return (alignment.astype(bf16).reshape(S, A, F), pair.astype(bf16).reshape(I, J, C))
 
 
 def solution(mesh):

time: 42.4 us -> 43 us (1.014)
  the two profiles are of different devices: /device:TPU:0 before, /device:TPU:11 now
where the time goes in v4:
time: 43 us; the launch traced here: 42.8 us
  Pallas kernels  37.4 us (87%)
  other arithmetic  3.31 us (8%)
  local copies, waits for them, and re-layouts  1.4 us (3%)
  between operations  0.65 us (2%)
    pallas_call x1, Pallas kernels, on_device(): pl.pallas_call(functools.partial(block_kernel, sizes, (S, A, F, H, I, J,...  37.4 us
    convert_element_type x1, other arithmetic, on_device(): pair.astype(bf16).reshape(I, J, C)  1.77 us
    convert_element_type x1, other arithmetic, on_device(): alignment.astype(bf16).reshape(S, A, F)  1.54 us
    unnamed x3, local copies, waits for them, and re-layouts  1.4 us

profile of v4, /device:TPU:11, one launch (start us, length us, event | category | flops | bytes accessed | tf_op | source)
XLA Modules:
  0.0 42.8 jit_solution(4169378578929020789)
XLA Ops:
  0.6 0.0 copy-start
  0.6 0.7 %copy-done = bf16[128,8]{0,1:T(8,128)(2,1)S(1)} copy-done((bf16[128,8]{0,1:T(8,128)(2,1)S(1)}, bf16[128,8]{0,1:T(8,128)(2,1)}, u32[]{:S(2)}) %copy-start) | copy-done | bytes 2072
  1.3 0.7 %copy.17.logit = bf16[128,8]{1,0:T(8,128)(2,1)} copy(bf16[128,8]{0,1:T(8,128)(2,1)S(1)} %copy-done) | data formatting | bytes 4096 | tf_op args[7]
  2.0 37.4 %block.1 = (f32[128,256]{1,0:T(8,128)}, f32[1024,128]{1,0:T(8,128)}) custom-call(bf16[128,256]{1,0:T(8,128)(2,1)} %bitcast.7, bf16[1024,128]{1,0:T(8,128)(2,1)} %bitcast.5, s32[4,32]{1,0:T(4,128)} %symbols.1, s32[4,32]{1,0:T(4,128)} %entries.1, s32[1,128]{1,0:T(1,128)} %bitcast.9, bf16[23,256]{1,0:T(8,128)(2,1)} %table.1, bf16[128,8]{1,0:T(8,128)(2,1)} %copy.17.logit, ...), custom_call_target="tpu_custom_call" | custom-call | tf_op jit(solution)/shard_map/block/pallas_call | solution.py:442
  39.5 1.5 %convert_element_type.6 = bf16[128,256]{1,0:T(8,128)(2,1)} convert(f32[128,256]{1,0:T(8,128)} %get-tuple-element.4) | non-fusion elementwise | flops 32768 | bytes 196608 | tf_op jit(solution)/shard_map/convert_element_type | solution.py:453
  41.0 1.8 %convert_element_type.7 = bf16[1024,128]{1,0:T(8,128)(2,1)} convert(f32[1024,128]{1,0:T(8,128)} %get-tuple-element.5) | non-fusion elementwise | flops 131072 | bytes 786432 | tf_op jit(solution)/shard_map/convert_element_type | solution.py:453
Async XLA Ops:
  0.6 0.7 %copy-start = (bf16[128,8]{0,1:T(8,128)(2,1)S(1)}, bf16[128,8]{0,1:T(8,128)(2,1)}, u32[]{:S(2)}) copy-start(bf16[128,8]{0,1:T(8,128)(2,1)} %param.22) | copy-start | bytes 6148
